TPU v7x, 32 devices: a whole 2x2x4 slice. The times are simulated.
32 devices in a mesh: fsdp: 16 (over z, y, core), tp: 2 (over x).
Axes of the slice: x: 2, y: 2, z: 4, core: 2. Of those that a mesh axis runs over, the one named last changes fastest.
Arguments:
- tokens: bfloat16 [16384, 1024], P(('fsdp', 'tp')), may hold values from -6 to 6
- norm_gains: bfloat16 [2, 1024], P(None, 'fsdp'), may hold values from 0.5 to 1.5
- query_weight: bfloat16 [1024, 1024], P('fsdp', 'tp'), may hold values from -0.1875 to 0.1875
- key_weight: bfloat16 [1024, 1024], P('fsdp', 'tp'), may hold values from -0.1875 to 0.1875
- value_weight: bfloat16 [1024, 1024], P('fsdp', 'tp'), may hold values from -0.1875 to 0.1875
- mix_gate_weight: bfloat16 [1024, 1024], P('fsdp', 'tp'), may hold values from -0.1875 to 0.1875
- output_weight: bfloat16 [1024, 1024], P('tp', 'fsdp'), may hold values from -0.5 to 0.5
- persistent_tokens: bfloat16 [32, 1024], P('fsdp', 'tp'), may hold values from -4 to 4
- memory_init: bfloat16 [1024, 256], P('tp', 'fsdp'), may hold values from -0.5 to 0.5
- gate_weight: bfloat16 [1024, 2816], P('fsdp', 'tp'), may hold values from -0.1875 to 0.1875
- up_weight: bfloat16 [1024, 2816], P('fsdp', 'tp'), may hold values from -0.1875 to 0.1875
- down_weight: bfloat16 [2816, 1024], P('tp', 'fsdp'), may hold values from -0.21875 to 0.21875
- doc_ids: int32 [16384], P('fsdp'), may hold values from 0 to 17, as said below
- span_starts: int32 [256], P('fsdp'), may hold values from 0 to 1, as said below
- memory_rates: float32 [3, 256, 8], P(None, 'fsdp', 'tp'), may hold values from 0.003 to 0.9, as said below
- out_grad: bfloat16 [16384, 1024], P(('fsdp', 'tp')), may hold values from -6 to 6
Outputs:
- output: bfloat16 [16384, 1024], P(('fsdp', 'tp'))
- tokens_grad: bfloat16 [16384, 1024], P(('fsdp', 'tp'))
- norm_gains_grad: float32 [2, 1024], P(None, 'fsdp')
- query_grad: float32 [1024, 1024], P('fsdp', 'tp')
- key_grad: float32 [1024, 1024], P('fsdp', 'tp')
- value_grad: float32 [1024, 1024], P('fsdp', 'tp')
- mix_gate_grad: float32 [1024, 1024], P('fsdp', 'tp')
- output_weight_grad: float32 [1024, 1024], P('tp', 'fsdp')
- persistent_grad: float32 [32, 1024], P('fsdp', 'tp')
- memory_init_grad: float32 [1024, 256], P('tp', 'fsdp')
- gate_grad: float32 [1024, 2816], P('fsdp', 'tp')
- up_grad: float32 [1024, 2816], P('fsdp', 'tp')
- down_grad: float32 [2816, 1024], P('tp', 'fsdp')
Inputs may be any that keep to these rules, and one draw needn't show every extreme that they name: `doc_ids`: within each sequence of 1024 tokens the numbers start at 0 and rise by one at each document start; every document but a sequence's last holds 60 to 800 tokens, and one holds exactly 800. Some sequence reaches the largest number that these lengths allow. span_starts[c] is 1 exactly when one of tokens c*64 to c*64 + 63 begins a sequence or has another document number than the token before it; so every sequence's first block has 1. memory_rates[0] holds momenta within 0.3 to 0.9, memory_rates[1] step sizes within 0.003 to 0.03, memory_rates[2] forgetting rates within 0.003 to 0.3.
All inputs are finite; a program needn't handle non-finite values.
Results may differ from a plain program's by a relative error of at most 0.022.
Values may be sent and summed in bfloat16 or wider, within the bound.
No kernel may reach another device: no remote copies, remote signals or barrier semaphores. Data moves between devices by JAX's collectives and lax.ppermute only.
A program may use at most 192 MiB of HBM per device.

v0:
```python
import jax
import jax.numpy as jnp
from jax import lax
from jax.sharding import PartitionSpec as P

HEAD = 128
PERSIST = 16
SEQ_LEN = 1024
SPAN = 64


EPSILON = 1e-05
MASKED_SCORE = -1e30


def matmul(left, right):
    return jnp.dot(left, right, preferred_element_type=jnp.float32)


def matmul_left(left, right):
    return lax.dot_general(
        left, right, (((0,), (0,)), ((), ())), preferred_element_type=jnp.float32
    )


def matmul_right(left, right):
    return lax.dot_general(
        left, right, (((1,), (1,)), ((), ())), preferred_element_type=jnp.float32
    )


def precise(left, right):
    return jnp.dot(left, right, precision=lax.Precision.HIGHEST)


def rms_norm(values, gain):
    return values * lax.rsqrt(jnp.mean(values * values, axis=-1, keepdims=True) + EPSILON) * gain


def memory_head(queries, key_rows, value_rows, documents, starts, rate_rows, init_one, init_two):
    spans = starts.shape[0]
    query_blocks = queries.reshape(spans, SPAN, HEAD)
    key_blocks = key_rows.reshape(spans, SPAN, HEAD)
    value_blocks = value_rows.reshape(spans, SPAN, HEAD)
    doc_blocks = documents.reshape(spans, SPAN)
    live_rows = (doc_blocks == doc_blocks[:, SPAN - 1 : SPAN]).astype(jnp.float32) / SPAN
    resets = starts.astype(jnp.float32)

    def advance(state, inputs):
        weight_one, weight_two, moment_one, moment_two = state
        query_block, key_block, value_block, live_block, reset_now, momentum, stepsize, forget = (
            inputs
        )
        weight_one = (1.0 - reset_now) * weight_one + reset_now * init_one
        weight_two = (1.0 - reset_now) * weight_two + reset_now * init_two
        moment_one = (1.0 - reset_now) * moment_one
        moment_two = (1.0 - reset_now) * moment_two
        readout = precise(jax.nn.silu(precise(query_block, weight_one)), weight_two)
        hidden = precise(key_block, weight_one)
        sigmoid_h = jax.nn.sigmoid(hidden)
        active = hidden * sigmoid_h
        errors = (precise(active, weight_two) - value_block) * live_block[:, None]
        grad_two = precise(active.T, errors)
        grad_one = precise(
            key_block.T,
            precise(errors, weight_two.T) * (sigmoid_h * (1.0 + hidden * (1.0 - sigmoid_h))),
        )
        moment_one = momentum * moment_one - stepsize * grad_one
        moment_two = momentum * moment_two - stepsize * grad_two
        weight_one = (1.0 - forget) * weight_one + moment_one
        weight_two = (1.0 - forget) * weight_two + moment_two
        return ((weight_one, weight_two, moment_one, moment_two), readout)

    zero_state = jnp.zeros((HEAD, HEAD), jnp.float32)
    finals, readout = lax.scan(
        jax.checkpoint(advance),
        (init_one, init_two, zero_state, zero_state),
        (
            query_blocks,
            key_blocks,
            value_blocks,
            live_rows,
            resets,
            rate_rows[0],
            rate_rows[1],
            rate_rows[2],
        ),
    )
    return readout.reshape(spans * SPAN, HEAD)


def memory_all(queries, key_rows, value_rows, memory_init, documents, starts, rate_rows):
    sequences = documents.shape[0] // SEQ_LEN
    head_count = queries.shape[1] // HEAD

    def by_head(values):
        return values.reshape(sequences, SEQ_LEN, head_count, HEAD).transpose(0, 2, 1, 3)

    weight_one = memory_init[:, :HEAD].reshape(head_count, HEAD, HEAD)
    weight_two = memory_init[:, HEAD:].reshape(head_count, HEAD, HEAD)
    per_rates = rate_rows.reshape(3, sequences, -1, head_count).transpose(1, 3, 0, 2)
    per_head = jax.vmap(memory_head, in_axes=(0, 0, 0, None, None, 0, 0, 0))
    per_sequence = jax.vmap(per_head, in_axes=(0, 0, 0, 0, 0, 0, None, None))
    readout = per_sequence(
        by_head(queries),
        by_head(key_rows),
        by_head(value_rows),
        documents.reshape(sequences, SEQ_LEN),
        starts.reshape(sequences, -1),
        per_rates,
        weight_one,
        weight_two,
    )
    return readout.transpose(0, 2, 1, 3).reshape(sequences * SEQ_LEN, head_count * HEAD)


def sequence_scores(queries, key_rows, fixed_keys, documents):
    scaling = HEAD ** (-0.5)
    scores = (
        jnp.einsum("qhd,khd->hqk", queries, key_rows, preferred_element_type=jnp.float32) * scaling
    )
    fixed_scores = (
        jnp.einsum("qhd,phd->hqp", queries, fixed_keys, preferred_element_type=jnp.float32)
        * scaling
    )
    places = jnp.arange(documents.shape[0])
    allowed = (documents[:, None] == documents[None, :]) & (places[None, :] <= places[:, None])
    return (jnp.where(allowed[None], scores, MASKED_SCORE), fixed_scores)


def attend_forward(queries, key_rows, value_rows, fixed_keys, fixed_values, documents):
    scores, fixed_scores = sequence_scores(queries, key_rows, fixed_keys, documents)
    highest = jnp.maximum(
        jnp.max(scores, axis=2, keepdims=True), jnp.max(fixed_scores, axis=2, keepdims=True)
    )
    weights = jnp.exp(scores - highest)
    fixed_weights = jnp.exp(fixed_scores - highest)
    totals = jnp.sum(weights, axis=2, keepdims=True) + jnp.sum(fixed_weights, axis=2, keepdims=True)
    result = jnp.einsum(
        "hqk,khd->qhd",
        (weights / totals).astype(jnp.bfloat16),
        value_rows,
        preferred_element_type=jnp.float32,
    )
    result = result + jnp.einsum(
        "hqp,phd->qhd",
        (fixed_weights / totals).astype(jnp.bfloat16),
        fixed_values,
        preferred_element_type=jnp.float32,
    )
    return (result, highest + jnp.log(totals))


def attend_backward(
    queries, key_rows, value_rows, fixed_keys, fixed_values, documents, log_total, attended_grad
):
    scaling = HEAD ** (-0.5)
    scores, fixed_scores = sequence_scores(queries, key_rows, fixed_keys, documents)
    probability = jnp.exp(scores - log_total)
    fixed_probability = jnp.exp(fixed_scores - log_total)
    prob_grad = jnp.einsum(
        "qhd,khd->hqk", attended_grad, value_rows, preferred_element_type=jnp.float32
    )
    fixed_prob_grad = jnp.einsum(
        "qhd,phd->hqp", attended_grad, fixed_values, preferred_element_type=jnp.float32
    )
    inner = jnp.sum(probability * prob_grad, axis=2, keepdims=True) + jnp.sum(
        fixed_probability * fixed_prob_grad, axis=2, keepdims=True
    )
    score_grad = (probability * (prob_grad - inner)).astype(jnp.bfloat16)
    fixed_score_grad = (fixed_probability * (fixed_prob_grad - inner)).astype(jnp.bfloat16)
    query_part = jnp.einsum(
        "hqk,khd->qhd", score_grad, key_rows, preferred_element_type=jnp.float32
    )
    query_part = scaling * (
        query_part
        + jnp.einsum(
            "hqp,phd->qhd", fixed_score_grad, fixed_keys, preferred_element_type=jnp.float32
        )
    )
    key_part = scaling * jnp.einsum(
        "hqk,qhd->khd", score_grad, queries, preferred_element_type=jnp.float32
    )
    value_part = jnp.einsum(
        "hqk,qhd->khd",
        probability.astype(jnp.bfloat16),
        attended_grad,
        preferred_element_type=jnp.float32,
    )
    fixed_key_part = scaling * jnp.einsum(
        "hqp,qhd->phd", fixed_score_grad, queries, preferred_element_type=jnp.float32
    )
    fixed_value_part = jnp.einsum(
        "hqp,qhd->phd",
        fixed_probability.astype(jnp.bfloat16),
        attended_grad,
        preferred_element_type=jnp.float32,
    )
    return (query_part, key_part, value_part, fixed_key_part, fixed_value_part)


def on_device(
    tokens,
    norm_gains,
    query_weight,
    key_weight,
    value_weight,
    mix_gate_weight,
    output_weight,
    persistent_tokens,
    memory_init,
    gate_weight,
    up_weight,
    down_weight,
    doc_ids,
    span_starts,
    memory_rates,
    out_grad,
):
    gains_all, w_query, w_key, w_value, w_mix, w_out, persist, mem_init, w_gate, w_up, w_down = (
        lax.all_gather(norm_gains, "fsdp", axis=1, tiled=True),
        lax.all_gather(query_weight, "fsdp", axis=0, tiled=True),
        lax.all_gather(key_weight, "fsdp", axis=0, tiled=True),
        lax.all_gather(value_weight, "fsdp", axis=0, tiled=True),
        lax.all_gather(mix_gate_weight, "fsdp", axis=0, tiled=True),
        lax.all_gather(output_weight, "fsdp", axis=1, tiled=True),
        lax.all_gather(persistent_tokens, "fsdp", axis=0, tiled=True),
        lax.all_gather(memory_init, "fsdp", axis=1, tiled=True),
        lax.all_gather(gate_weight, "fsdp", axis=0, tiled=True),
        lax.all_gather(up_weight, "fsdp", axis=0, tiled=True),
        lax.all_gather(down_weight, "fsdp", axis=1, tiled=True),
    )
    gains = gains_all.astype(jnp.float32)
    rows_in = tokens.astype(jnp.float32)
    normed = rms_norm(rows_in, gains[0]).astype(jnp.bfloat16)
    normed_all = lax.all_gather(normed, "tp", axis=0, tiled=True)
    queries = matmul(normed_all, w_query).astype(jnp.bfloat16)
    key_rows = matmul(normed_all, w_key).astype(jnp.bfloat16)
    value_rows = matmul(normed_all, w_value).astype(jnp.bfloat16)
    gate_pre = matmul(normed_all, w_mix)
    group_rows = normed_all.shape[0]
    head_count = queries.shape[1] // HEAD
    sequences = group_rows // SEQ_LEN

    def by_head(values):
        return values.reshape(sequences, SEQ_LEN, head_count, HEAD)

    fixed_keys = persist[:PERSIST].reshape(PERSIST, head_count, HEAD)
    fixed_values = persist[PERSIST:].reshape(PERSIST, head_count, HEAD)
    doc_rows = doc_ids.reshape(sequences, SEQ_LEN)

    def forward_one(inputs):
        return attend_forward(inputs[0], inputs[1], inputs[2], fixed_keys, fixed_values, inputs[3])

    attended, log_totals = lax.map(
        forward_one, (by_head(queries), by_head(key_rows), by_head(value_rows), doc_rows)
    )
    attended = attended.reshape(group_rows, head_count * HEAD)

    def recall(query_vals, key_vals, value_vals, init_vals):
        return memory_all(
            query_vals, key_vals, value_vals, init_vals, doc_ids, span_starts, memory_rates
        )

    recalled, recall_back = jax.vjp(
        recall,
        queries.astype(jnp.float32),
        key_rows.astype(jnp.float32),
        value_rows.astype(jnp.float32),
        mem_init.astype(jnp.float32),
    )
    gate_open = jax.nn.sigmoid(gate_pre)
    combined = (attended + gate_open * recalled).astype(jnp.bfloat16)
    branch = lax.psum_scatter(
        matmul(combined, w_out).astype(jnp.bfloat16), "tp", scatter_dimension=0, tiled=True
    ).astype(jnp.float32)
    hidden_one = rows_in + branch
    normed_two = rms_norm(hidden_one, gains[1]).astype(jnp.bfloat16)
    normed_two_all, grad_rows = (
        lax.all_gather(normed_two, "tp", axis=0, tiled=True),
        lax.all_gather(out_grad, "tp", axis=0, tiled=True),
    )
    gate_rows = matmul(normed_two_all, w_gate)
    up_rows = matmul(normed_two_all, w_up)
    hidden = (jax.nn.silu(gate_rows) * up_rows).astype(jnp.bfloat16)
    ffn_branch = lax.psum_scatter(
        matmul(hidden, w_down).astype(jnp.bfloat16), "tp", scatter_dimension=0, tiled=True
    ).astype(jnp.float32)
    output = (hidden_one + ffn_branch).astype(jnp.bfloat16)
    down_grad = matmul_left(hidden, grad_rows)
    hidden_grad = matmul_right(grad_rows, w_down)
    gate_sigmoid = jax.nn.sigmoid(gate_rows)
    gate_back = (
        hidden_grad * up_rows * gate_sigmoid * (1.0 + gate_rows * (1.0 - gate_sigmoid))
    ).astype(jnp.bfloat16)
    up_back = (hidden_grad * jax.nn.silu(gate_rows)).astype(jnp.bfloat16)
    gate_grad = matmul_left(normed_two_all, gate_back)
    up_grad = matmul_left(normed_two_all, up_back)
    normed_two_grad = lax.psum_scatter(
        (matmul_right(gate_back, w_gate) + matmul_right(up_back, w_up)).astype(jnp.bfloat16),
        "tp",
        scatter_dimension=0,
        tiled=True,
    ).astype(jnp.float32)
    unused_two, norm_two_back = jax.vjp(rms_norm, hidden_one, gains[1])
    hidden_one_grad, gain_two_grad = norm_two_back(normed_two_grad)
    hidden_one_grad = out_grad.astype(jnp.float32) + hidden_one_grad
    branch_grad = hidden_one_grad.astype(jnp.bfloat16)
    branch_rows = lax.all_gather(branch_grad, "tp", axis=0, tiled=True)
    out_weight_grad = matmul_left(combined, branch_rows)
    combined_grad = matmul_right(branch_rows, w_out)
    attended_grad = combined_grad.astype(jnp.bfloat16)
    gate_pre_grad = (combined_grad * recalled * gate_open * (1.0 - gate_open)).astype(jnp.bfloat16)
    recalled_grad = combined_grad * gate_open

    def backward_one(inputs):
        return attend_backward(
            inputs[0],
            inputs[1],
            inputs[2],
            fixed_keys,
            fixed_values,
            inputs[3],
            inputs[4],
            inputs[5],
        )

    query_att, key_att, value_att, fixed_key_att, fixed_value_att = lax.map(
        backward_one,
        (
            by_head(queries),
            by_head(key_rows),
            by_head(value_rows),
            doc_rows,
            log_totals,
            by_head(attended_grad),
        ),
    )
    query_mem, key_mem, value_mem, mem_init_grad = recall_back(recalled_grad)
    width_local = head_count * HEAD
    query_back = (query_att.reshape(group_rows, width_local) + query_mem).astype(jnp.bfloat16)
    key_back = (key_att.reshape(group_rows, width_local) + key_mem).astype(jnp.bfloat16)
    value_back = (value_att.reshape(group_rows, width_local) + value_mem).astype(jnp.bfloat16)
    persist_grad = jnp.concatenate(
        [
            jnp.sum(fixed_key_att, axis=0).reshape(PERSIST, width_local),
            jnp.sum(fixed_value_att, axis=0).reshape(PERSIST, width_local),
        ],
        axis=0,
    )
    query_grad = matmul_left(normed_all, query_back)
    key_grad = matmul_left(normed_all, key_back)
    value_grad = matmul_left(normed_all, value_back)
    mix_grad = matmul_left(normed_all, gate_pre_grad)
    total = matmul_right(query_back, w_query)
    total = total + matmul_right(key_back, w_key)
    total = total + matmul_right(value_back, w_value)
    normed_grad = lax.psum_scatter(
        (total + matmul_right(gate_pre_grad, w_mix)).astype(jnp.bfloat16),
        "tp",
        scatter_dimension=0,
        tiled=True,
    ).astype(jnp.float32)
    unused_one, norm_one_back = jax.vjp(rms_norm, rows_in, gains[0])
    input_grad, gain_one_grad = norm_one_back(normed_grad)
    tokens_grad = (hidden_one_grad + input_grad).astype(jnp.bfloat16)
    gain_terms = lax.psum(jnp.stack([gain_one_grad, gain_two_grad]), "tp")
    (
        gains_grad,
        query_out,
        key_out,
        value_out,
        mix_out,
        out_weight_out,
        persist_out,
        mem_init_out,
        gate_out,
        up_out,
        down_out,
    ) = (
        lax.psum_scatter(
            gain_terms.astype(jnp.bfloat16), "fsdp", scatter_dimension=1, tiled=True
        ).astype(jnp.float32),
        lax.psum_scatter(
            query_grad.astype(jnp.bfloat16), "fsdp", scatter_dimension=0, tiled=True
        ).astype(jnp.float32),
        lax.psum_scatter(
            key_grad.astype(jnp.bfloat16), "fsdp", scatter_dimension=0, tiled=True
        ).astype(jnp.float32),
        lax.psum_scatter(
            value_grad.astype(jnp.bfloat16), "fsdp", scatter_dimension=0, tiled=True
        ).astype(jnp.float32),
        lax.psum_scatter(
            mix_grad.astype(jnp.bfloat16), "fsdp", scatter_dimension=0, tiled=True
        ).astype(jnp.float32),
        lax.psum_scatter(
            out_weight_grad.astype(jnp.bfloat16), "fsdp", scatter_dimension=1, tiled=True
        ).astype(jnp.float32),
        lax.psum_scatter(
            persist_grad.astype(jnp.bfloat16), "fsdp", scatter_dimension=0, tiled=True
        ).astype(jnp.float32),
        lax.psum_scatter(
            mem_init_grad.astype(jnp.bfloat16), "fsdp", scatter_dimension=1, tiled=True
        ).astype(jnp.float32),
        lax.psum_scatter(
            gate_grad.astype(jnp.bfloat16), "fsdp", scatter_dimension=0, tiled=True
        ).astype(jnp.float32),
        lax.psum_scatter(
            up_grad.astype(jnp.bfloat16), "fsdp", scatter_dimension=0, tiled=True
        ).astype(jnp.float32),
        lax.psum_scatter(
            down_grad.astype(jnp.bfloat16), "fsdp", scatter_dimension=1, tiled=True
        ).astype(jnp.float32),
    )
    return (
        output,
        tokens_grad,
        gains_grad,
        query_out,
        key_out,
        value_out,
        mix_out,
        out_weight_out,
        persist_out,
        mem_init_out,
        gate_out,
        up_out,
        down_out,
    )


def solution(mesh):
    placed = (
        P(("fsdp", "tp"), None),
        P(None, "fsdp"),
        P("fsdp", "tp"),
        P("fsdp", "tp"),
        P("fsdp", "tp"),
        P("fsdp", "tp"),
        P("tp", "fsdp"),
        P("fsdp", "tp"),
        P("tp", "fsdp"),
        P("fsdp", "tp"),
        P("fsdp", "tp"),
        P("tp", "fsdp"),
        P("fsdp"),
        P("fsdp"),
        P(None, "fsdp", "tp"),
        P(("fsdp", "tp"), None),
    )
    return jax.shard_map(
        on_device,
        mesh=mesh,
        in_specs=placed,
        out_specs=(
            P(("fsdp", "tp"), None),
            P(("fsdp", "tp"), None),
            P(None, "fsdp"),
            P("fsdp", "tp"),
            P("fsdp", "tp"),
            P("fsdp", "tp"),
            P("fsdp", "tp"),
            P("tp", "fsdp"),
            P("fsdp", "tp"),
            P("tp", "fsdp"),
            P("fsdp", "tp"),
            P("fsdp", "tp"),
            P("tp", "fsdp"),
        ),
        check_vma=False,
    )
```

profile of v0, /device:TPU:0, one launch (start us, length us, event | category | flops | bytes accessed | tf_op | source)
XLA Modules:
  0.0 1723.6 jit_solution(9869631278972660051)
XLA Ops:
  8.0 23.3 %all-gather = bf16[16,64,2]{1,2,0:T(2,128)(2,1)S(1)} all-gather(bf16[1,64,2]{1,2,0:T(2,128)(2,1)} %bitcast.787), channel_id=1, replica_groups=mesh['fsdp'=16,'tp'=2] {'fsdp'}, dimensions={0}, use_global_device_ids=true | all-gather | bytes 4352 | tf_op jit(solution)/shard_map/all_gather | solution.py:221
  40.3 17.5 %all-gather.1 = bf16[16,2,512]{2,1,0:T(2,128)(2,1)S(1)} all-gather(bf16[1,2,512]{2,1,0:T(2,128)(2,1)S(1)} %bitcast.786), channel_id=1, replica_groups=mesh['fsdp'=16,'tp'=2] {'fsdp'}, dimensions={0}, use_global_device_ids=true | all-gather | bytes 34816 | tf_op jit(solution)/shard_map/all_gather | solution.py:227
  58.0 19.5 %all_gather.52 = bf16[512,256]{0,1:T(8,128)(2,1)S(1)} all-gather(bf16[512,16]{0,1:T(8,128)(2,1)S(1)} %copy-done.51), channel_id=1, replica_groups=mesh['fsdp'=16,'tp'=2] {'fsdp'}, dimensions={1}, use_global_device_ids=true | all-gather | bytes 278528 | tf_op jit(solution)/shard_map/all_gather | solution.py:228
  78.3 6.7 all-gather.15.cloned.1.call-done
  88.5 36.6 %all-gather.21.cloned.1.call-done = bf16[1024,512]{1,0:T(8,128)(2,1)} async-done(((bf16[64,512]{1,0:T(8,128)(2,1)}), bf16[1024,512]{1,0:T(8,128)(2,1)}) %all-gather.21.cloned.1.call-update) | async-done | bytes 1048592 | tf_op jit(solution)/shard_map/all_gather | solution.py:223
  128.4 8.0 fusion.182
  136.3 8.0 fusion.128
  150.1 13.9 all-gather.17.cloned.1.call-done
  164.0 4.1 convolution_convert_fusion.12
  180.2 190.0 %while.19 = (s32[]{:T(128)}, f32[1,4,128,128]{3,2,1,0:T(8,128)S(1)}, f32[1,4,128,128]{3,2,1,0:T(8,128)S(1)}, f32[1,4,128,128]{3,2,1,0:T(8,128)S(1)}, f32[1,4,128...) while((s32[]{:T(128)}, ...), condition=%wide.region_6.7_spmd.clone, body=%wide.region_5.6_spmd.clone.sunk | while | flops 354353152 | bytes 8392860 | solution.py:75
  374.5 9.6 bitcast_add_fusion.8
  384.1 6.1 fusion.154
  391.2 3.8 convolution_convert_fusion.4
  395.9 30.3 %reduce-scatter.17.cloned.1.call-done = bf16[512,1024]{1,0:T(8,128)(2,1)} async-done(((bf16[1024,1024]{1,0:T(8,128)(2,1)}), bf16[512,1024]{1,0:T(8,128)(2,1)}) %reduce-scatter.17.cloned.1.call-update) | async-done | bytes 1048592 | tf_op jit(solution)/shard_map/reduce_scatter | solution.py:274
  431.3 41.1 %all-gather.29.cloned.1.call-done = bf16[1024,1408]{1,0:T(8,128)(2,1)} async-done(((bf16[64,1408]{1,0:T(8,128)(2,1)}), bf16[1024,1408]{1,0:T(8,128)(2,1)}) %all-gather.29.cloned.1.call-update) | async-done | bytes 2883600 | tf_op jit(solution)/shard_map/all_gather | solution.py:229
  472.4 33.3 %all-gather.27.cloned.1.call-done = bf16[1024,1024]{1,0:T(8,128)(2,1)} async-done(((bf16[512,1024]{1,0:T(8,128)(2,1)}), bf16[1024,1024]{1,0:T(8,128)(2,1)}) %all-gather.27.cloned.1.call-update) | async-done | bytes 2097168 | tf_op jit(solution)/shard_map/all_gather | solution.py:280
  505.7 8.4 fusion.184
  514.1 37.8 %all-gather.31.cloned.1.call-done = bf16[1024,1408]{1,0:T(8,128)(2,1)} async-done(((bf16[64,1408]{1,0:T(8,128)(2,1)}), bf16[1024,1408]{1,0:T(8,128)(2,1)}) %all-gather.31.cloned.1.call-update) | async-done | bytes 2883600 | tf_op jit(solution)/shard_map/all_gather | solution.py:230
  551.9 8.3 fusion.185
  560.2 25.0 %all-gather.35.cloned.1.call-done = bf16[1024,1024]{1,0:T(8,128)(2,1)} async-done(((bf16[512,1024]{1,0:T(8,128)(2,1)}), bf16[1024,1024]{1,0:T(8,128)(2,1)}) %all-gather.35.cloned.1.call-update) | async-done | bytes 2097168 | tf_op jit(solution)/shard_map/all_gather | solution.py:281
  585.2 46.1 %all-gather.33.cloned.1.call-done = bf16[1408,1024]{0,1:T(8,128)(2,1)} async-done(((bf16[1408,64]{0,1:T(8,128)(2,1)}), bf16[1408,1024]{0,1:T(8,128)(2,1)}) %all-gather.33.cloned.1.call-update) | async-done | bytes 2883600 | tf_op jit(solution)/shard_map/all_gather | solution.py:231
  631.3 11.4 multiply_convert_fusion.1
  646.7 4.7 add_convert_fusion.1
  651.4 30.6 %reduce-scatter.21.cloned.1.call-done = bf16[512,1024]{1,0:T(8,128)(2,1)} async-done(((bf16[1024,1024]{1,0:T(8,128)(2,1)}), bf16[512,1024]{1,0:T(8,128)(2,1)}) %reduce-scatter.21.cloned.1.call-update) | async-done | bytes 1048592 | tf_op jit(solution)/shard_map/reduce_scatter | solution.py:299
  686.9 7.5 convolution_convert_fusion.2
  694.7 7.8 convolution_convert_fusion.1
  704.3 7.5 convolution_convert_fusion
  711.9 8.2 all-gather.37.cloned.1.call-done
  720.1 6.4 fusion.157
  734.5 459.5 %while.20 = (s32[]{:T(128)}, f32[4,128,128]{1,2,0:T(8,128)S(1)}, f32[4,128,128]{1,2,0:T(8,128)S(1)}, f32[1,4,128,128]{2,3,1,0:T(8,128)}, f32[1,4,128,128]{2,3,1,...) while((s32[]{:T(128)}, f32[4,128,128]{1,2,0:T(8,128)S(1)}, ...), condition=%wide.region_15.16_spmd.clone, body=%wide.region_14.15_spmd.clone.sunk | while | flops 911278080 | bytes 26479580 | solution.py:75
  1200.5 10.8 multiply_reduce_fusion
  1212.1 12.0 multiply_convert_fusion
  1227.5 4.2 convolution_multiply_fusion.3
  1244.7 4.3 convolution_convert_fusion.5
  1249.1 5.0 fusion.187
  1260.1 7.7 fusion.130
  1272.1 4.1 convolution_convert_fusion.6
  1285.2 7.4 convolution_convert_fusion.3
  1300.9 61.2 %all-reduce.2 = bf16[32,512]{1,0:T(8,128)(2,1)S(1)} all-reduce(bf16[32,512]{1,0:T(8,128)(2,1)S(1)} %pad_maximum_fusion), channel_id=12, replica_groups=mesh['fsdp'=16,'tp'=2] {'fsdp'}, use_global_device_ids=true, to_apply=%region_27.28.clone | all-reduce | flops 16384 | bytes 65536
  1365.5 42.6 %reduce-scatter.33.cloned.1.call-done = bf16[512,64]{0,1:T(8,128)(2,1)} async-done(((bf16[512,1024]{0,1:T(8,128)(2,1)}), bf16[512,64]{0,1:T(8,128)(2,1)}) %reduce-scatter.33.cloned.1.call-update) | async-done | bytes 65552 | tf_op jit(solution)/shard_map/reduce_scatter | solution.py:396
  1409.6 58.8 %reduce-scatter.25.cloned.1.call-done = bf16[64,512]{1,0:T(8,128)(2,1)} async-done(((bf16[1024,512]{1,0:T(8,128)(2,1)}), bf16[64,512]{1,0:T(8,128)(2,1)}) %reduce-scatter.25.cloned.1.call-update) | async-done | bytes 65552 | tf_op jit(solution)/shard_map/reduce_scatter | solution.py:384
  1469.9 58.8 %reduce-scatter.29.cloned.1.call-done = bf16[64,512]{1,0:T(8,128)(2,1)} async-done(((bf16[1024,512]{1,0:T(8,128)(2,1)}), bf16[64,512]{1,0:T(8,128)(2,1)}) %reduce-scatter.29.cloned.1.call-update) | async-done | bytes 65552 | tf_op jit(solution)/shard_map/reduce_scatter | solution.py:390
  1530.2 58.9 %reduce-scatter.31.cloned.1.call-done = bf16[64,512]{1,0:T(8,128)(2,1)} async-done(((bf16[1024,512]{1,0:T(8,128)(2,1)}), bf16[64,512]{1,0:T(8,128)(2,1)}) %reduce-scatter.31.cloned.1.call-update) | async-done | bytes 65552 | tf_op jit(solution)/shard_map/reduce_scatter | solution.py:393
  1590.6 31.5 %reduce-scatter.23.cloned.1.call-done = bf16[512,1024]{1,0:T(8,128)(2,1)} async-done(((bf16[1024,1024]{1,0:T(8,128)(2,1)}), bf16[512,1024]{1,0:T(8,128)(2,1)}) %reduce-scatter.23.cloned.1.call-update) | async-done | bytes 1048592 | tf_op jit(solution)/shard_map/reduce_scatter | solution.py:358
  1624.3 5.0 psum.7
  1630.2 26.1 %reduce-scatter.19.cloned.1.call-done = bf16[512,1024]{1,0:T(8,128)(2,1)} async-done(((bf16[1024,1024]{1,0:T(8,128)(2,1)}), bf16[512,1024]{1,0:T(8,128)(2,1)}) %reduce-scatter.19.cloned.1.call-update) | async-done | bytes 1048592 | tf_op jit(solution)/shard_map/reduce_scatter | solution.py:286
  1656.3 4.1 fusion.146
  1660.4 55.0 %reduce-scatter.43.cloned.1.call-done = bf16[64,2]{1,0:T(8,128)(2,1)} async-done(((bf16[1024,2]{1,0:T(8,128)(2,1)}), bf16[64,2]{1,0:T(8,128)(2,1)}) %reduce-scatter.43.cloned.1.call-update) | async-done | bytes 272
  (1300 shorter events, 764.5 us)
Async XLA Ops:
  7.2 71.1 %all-gather.19.cloned.1.call-start = ((), (), s32[]{:S(2)}) async-start(), calls=%async_computation.16 | async-start | bytes 1114112 | tf_op jit(solution)/shard_map/all_gather | solution.py:222
  7.9 77.1 %all-gather.15.cloned.1.call-start = ((), (), s32[]{:S(2)}) async-start(), calls=%async_computation.14 | async-start | bytes 3145728 | tf_op jit(solution)/shard_map/all_gather | solution.py:236
  33.5 651.5 %copy-start.35 = (f32[1,1024]{1,0:T(1,128)}, f32[1,1024]{1,0:T(1,128)S(1)}, u32[]{:S(2)}) copy-start(f32[1,1024]{1,0:T(1,128)S(1)} %get-tuple-element.1134) | copy-start | bytes 12292
  33.5 24.4 %copy-start.51 = (bf16[512,16]{0,1:T(8,128)(2,1)S(1)}, bf16[512,16]{0,1:T(8,128)(2,1)}, u32[]{:S(2)}) copy-start(bf16[512,16]{0,1:T(8,128)(2,1)} %param.28) | copy-start | bytes 49156
  36.0 89.1 %all-gather.21.cloned.1.call-start = ((), (), s32[]{:S(2)}) async-start(), calls=%async_computation.17 | async-start | bytes 1114112 | tf_op jit(solution)/shard_map/all_gather | solution.py:223
  36.8 127.2 %all-gather.17.cloned.1.call-start = ((), (), s32[]{:S(2)}) async-start(), calls=%async_computation.15 | async-start | bytes 1114112 | tf_op jit(solution)/shard_map/all_gather | solution.py:224
  37.3 346.8 %all-gather.23.cloned.1.call-start = ((), (), s32[]{:S(2)}) async-start(), calls=%async_computation.18 | async-start | bytes 1114112 | tf_op jit(solution)/shard_map/all_gather | solution.py:225
  37.9 352.3 %all-gather.25.cloned.1.call-start = ((), (), s32[]{:S(2)}) async-start(), calls=%async_computation.19 | async-start | bytes 1114112 | tf_op jit(solution)/shard_map/all_gather | solution.py:226
  38.5 39.2 %copy-start.57 = (f32[3,16,4]{1,2,0:T(4,128)S(1)}, f32[3,16,4]{1,2,0:T(4,128)}, u32[]{:S(2)}) copy-start(f32[3,16,4]{1,2,0:T(4,128)} %param.34) | copy-start | bytes 2308
  38.5 39.6 %copy-start.66 = (s32[16]{0:T(128)S(1)}, s32[16]{0:T(128)}, u32[]{:S(2)}) copy-start(s32[16]{0:T(128)} %param.33) | copy-start | bytes 196
  38.5 387.6 %reduce-scatter.17.cloned.1.call-start = ((), (), s32[]{:S(2)}) async-start(), calls=%async_computation.20 | async-start | bytes 3145728 | tf_op jit(solution)/shard_map/reduce_scatter | solution.py:274
  57.9 30.3 %copy-start.30 = (bf16[16,4,128]{2,1,0:T(4,128)(2,1)}, bf16[16,4,128]{2,1,0:T(4,128)(2,1)S(1)}, u32[]{:S(2)}) copy-start(bf16[16,4,128]{2,1,0:T(4,128)(2,1)S(1)} %reshape.828) | copy-start | bytes 49156
  57.9 315.4 %copy-start.32 = (bf16[16,4,128]{2,1,0:T(4,128)(2,1)}, bf16[16,4,128]{2,1,0:T(4,128)(2,1)S(1)}, u32[]{:S(2)}) copy-start(bf16[16,4,128]{2,1,0:T(4,128)(2,1)S(1)} %reshape.829) | copy-start | bytes 49156
  88.2 85.7 %copy-start.2 = (bf16[1024,512]{0,1:T(8,128)(2,1)}, bf16[1024,512]{0,1:T(8,128)(2,1)S(1)}, u32[]{:S(2)}) copy-start(bf16[1024,512]{0,1:T(8,128)(2,1)S(1)} %convolution_convert_fusion.11) | copy-start | bytes 3145732
  88.5 284.8 %copy-start.10 = (f32[4,1024,16]{1,2,0:T(8,128)}, f32[4,1024,16]{1,2,0:T(8,128)S(1)}, u32[]{:S(2)}) copy-start(f32[4,1024,16]{1,2,0:T(8,128)S(1)} %get-tuple-element.1142) | copy-start | bytes 786436
  395.1 31.1 %copy-start.1 = (bf16[512,1024]{1,0:T(8,128)(2,1)S(1)}, bf16[512,1024]{1,0:T(8,128)(2,1)}, u32[]{:S(2)}) copy-start(bf16[512,1024]{1,0:T(8,128)(2,1)} %param.20) | copy-start | bytes 3145732
  395.1 77.3 %all-gather.29.cloned.1.call-start = ((), (), s32[]{:S(2)}) async-start(), calls=%async_computation.22 | async-start | bytes 3063808 | tf_op jit(solution)/shard_map/all_gather | solution.py:229
  395.8 109.9 %all-gather.27.cloned.1.call-start = ((), (), s32[]{:S(2)}) async-start(), calls=%async_computation.21 | async-start | bytes 3145728 | tf_op jit(solution)/shard_map/all_gather | solution.py:280
  427.9 257.1 %copy-start.41 = (f32[512]{0:T(512)}, f32[512]{0:T(512)S(1)}, u32[]{:S(2)}) copy-start(f32[512]{0:T(512)S(1)} %fusion.176) | copy-start | bytes 6148
  429.3 122.5 %all-gather.31.cloned.1.call-start = ((), (), s32[]{:S(2)}) async-start(), calls=%async_computation.23 | async-start | bytes 3063808 | tf_op jit(solution)/shard_map/all_gather | solution.py:230
  429.9 155.2 %all-gather.35.cloned.1.call-start = ((), (), s32[]{:S(2)}) async-start(), calls=%async_computation.26 | async-start | bytes 3145728 | tf_op jit(solution)/shard_map/all_gather | solution.py:281
  430.7 200.6 %all-gather.33.cloned.1.call-start = ((), (), s32[]{:S(2)}) async-start(), calls=%async_computation.24 | async-start | bytes 3063808 | tf_op jit(solution)/shard_map/all_gather | solution.py:231
  431.2 250.8 %reduce-scatter.21.cloned.1.call-start = ((), (), s32[]{:S(2)}) async-start(), calls=%async_computation.27 | async-start | bytes 3145728 | tf_op jit(solution)/shard_map/reduce_scatter | solution.py:299
  631.3 11.5 copy-start.59
  651.3 68.7 %all-gather.37.cloned.1.call-start = ((), (), s32[]{:S(2)}) async-start(), calls=%async_computation.28 | async-start | bytes 3145728 | tf_op jit(solution)/shard_map/all_gather | solution.py:309
  686.8 608.1 %reduce-scatter.37.cloned.1.call-start = ((), (), s32[]{:S(2)}) async-start(), calls=%async_computation.36 | async-start | bytes 3063808 | tf_op jit(solution)/shard_map/reduce_scatter | solution.py:405
  694.4 602.2 %reduce-scatter.39.cloned.1.call-start = ((), (), s32[]{:S(2)}) async-start(), calls=%async_computation.37 | async-start | bytes 3063808 | tf_op jit(solution)/shard_map/reduce_scatter | solution.py:408
  702.5 595.8 %reduce-scatter.41.cloned.1.call-start = ((), (), s32[]{:S(2)}) async-start(), calls=%async_computation.38 | async-start | bytes 3063808 | tf_op jit(solution)/shard_map/reduce_scatter | solution.py:411
  711.8 650.8 %reduce-scatter.35.cloned.1.call-start = ((), (), s32[]{:S(2)}) async-start(), calls=%async_computation.35 | async-start | bytes 278528 | tf_op jit(solution)/shard_map/reduce_scatter | solution.py:402
  1211.3 12.8 copy-start.34
  1212.1 15.4 copy-start.3
  1231.7 132.3 %reduce-scatter.27.cloned.1.call-start = ((), (), s32[]{:S(2)}) async-start(), calls=%async_computation.31 | async-start | bytes 1114112 | tf_op jit(solution)/shard_map/reduce_scatter | solution.py:387
  1237.8 170.3 %reduce-scatter.33.cloned.1.call-start = ((), (), s32[]{:S(2)}) async-start(), calls=%async_computation.34 | async-start | bytes 1114112 | tf_op jit(solution)/shard_map/reduce_scatter | solution.py:396
  1249.0 219.4 %reduce-scatter.25.cloned.1.call-start = ((), (), s32[]{:S(2)}) async-start(), calls=%async_computation.30 | async-start | bytes 1114112 | tf_op jit(solution)/shard_map/reduce_scatter | solution.py:384
  1260.0 268.7 %reduce-scatter.29.cloned.1.call-start = ((), (), s32[]{:S(2)}) async-start(), calls=%async_computation.32 | async-start | bytes 1114112 | tf_op jit(solution)/shard_map/reduce_scatter | solution.py:390
  1272.1 317.0 %reduce-scatter.31.cloned.1.call-start = ((), (), s32[]{:S(2)}) async-start(), calls=%async_computation.33 | async-start | bytes 1114112 | tf_op jit(solution)/shard_map/reduce_scatter | solution.py:393
  1276.2 345.9 %reduce-scatter.23.cloned.1.call-start = ((), (), s32[]{:S(2)}) async-start(), calls=%async_computation.29 | async-start | bytes 3145728 | tf_op jit(solution)/shard_map/reduce_scatter | solution.py:358
  1285.2 371.1 %reduce-scatter.19.cloned.1.call-start = ((), (), s32[]{:S(2)}) async-start(), calls=%async_computation.25 | async-start | bytes 3145728 | tf_op jit(solution)/shard_map/reduce_scatter | solution.py:286
  1292.7 422.7 %reduce-scatter.43.cloned.1.call-start = ((), (), s32[]{:S(2)}) async-start(), calls=%async_computation.39 | async-start | bytes 278528
  1300.4 321.7 %copy-start.38 = (f32[1,1024]{1,0:T(1,128)S(1)}, f32[1,1024]{1,0:T(1,128)}, u32[]{:S(2)}) copy-start(f32[1,1024]{1,0:T(1,128)} %copy-done.37) | copy-start | bytes 12292
  1300.4 321.7 %copy-start.44 = (f32[512]{0:T(512)S(1)}, f32[512]{0:T(512)}, u32[]{:S(2)}) copy-start(f32[512]{0:T(512)} %copy-done.43) | copy-start | bytes 6148
  1300.4 323.8 %copy-start.50 = (f32[1024]{0:T(1024)S(1)}, f32[1024]{0:T(1024)}, u32[]{:S(2)}) copy-start(f32[1024]{0:T(1024)} %get-tuple-element.1005) | copy-start | bytes 12292
  1300.8 329.4 %copy-start.47 = (f32[512]{0:T(512)S(1)}, f32[512]{0:T(512)}, u32[]{:S(2)}) copy-start(f32[512]{0:T(512)} %copy-done.46) | copy-start | bytes 6148
  1300.8 355.5 %copy-start.5 = (bf16[512,1024]{1,0:T(8,128)(2,1)S(1)}, bf16[512,1024]{1,0:T(8,128)(2,1)}, u32[]{:S(2)}) copy-start(bf16[512,1024]{1,0:T(8,128)(2,1)} %reduce-scatter.17.cloned.1.call-done) | copy-start | bytes 3145732
  1300.8 355.5 %copy-start.13 = (bf16[512,1024]{1,0:T(8,128)(2,1)S(1)}, bf16[512,1024]{1,0:T(8,128)(2,1)}, u32[]{:S(2)}) copy-start(bf16[512,1024]{1,0:T(8,128)(2,1)} %param.35) | copy-start | bytes 3145732
  1300.8 355.5 %copy-start.36 = (f32[1,1024]{1,0:T(1,128)S(1)}, f32[1,1024]{1,0:T(1,128)}, u32[]{:S(2)}) copy-start(f32[1,1024]{1,0:T(1,128)} %copy-done.35) | copy-start | bytes 12292
  1300.8 355.5 %copy-start.42 = (f32[512]{0:T(512)S(1)}, f32[512]{0:T(512)}, u32[]{:S(2)}) copy-start(f32[512]{0:T(512)} %copy-done.41) | copy-start | bytes 6148
  1300.8 355.5 %copy-start.49 = (f32[512]{0:T(512)S(1)}, f32[512]{0:T(512)}, u32[]{:S(2)}) copy-start(f32[512]{0:T(512)} %copy-done.48) | copy-start | bytes 6148
  (154 other events, 574.7 us)
Sparse Core Ops, SparseCore 0:
  10.1 40.6 all-gather.18
  52.9 32.0 all-gather.14
  87.2 37.8 all-gather.20
  127.1 36.8 all-gather.16
  166.0 36.8 all-gather.22
  204.9 36.8 all-gather.24
  395.2 30.8 reduce-scatter.16
  428.4 43.9 all-gather.28
  474.0 31.7 all-gather.26
  507.9 43.9 all-gather.30
  553.4 31.7 all-gather.34
  587.3 43.9 all-gather.32
  651.5 30.5 reduce-scatter.20
  686.9 33.0 all-gather.36
  723.7 65.2 reduce-scatter.36
  792.6 64.2 reduce-scatter.38
  860.6 64.3 reduce-scatter.40
  1231.8 55.7 reduce-scatter.34
  1291.3 56.7 reduce-scatter.26
  1351.5 56.5 reduce-scatter.32
  1411.7 56.6 reduce-scatter.24
  1472.1 56.6 reduce-scatter.28
  1532.4 56.6 reduce-scatter.30
  1591.2 30.8 reduce-scatter.22
  1624.3 31.9 reduce-scatter.18
  1659.7 55.6 reduce-scatter.42
where the time goes:
time: 1730 us; the launch traced here: 1720 us
  waiting for transfers between devices  647 us (37%)
  matrix products  511 us (30%)
  local copies, waits for them, and re-layouts  226 us (13%)
  other arithmetic  182 us (11%)
  blocking collectives  127 us (7%)
    dot_general x400, matrix products, precise(): return jnp.dot(left, right, precision=lax.Precision.HIGHEST)  346 us
    squeeze x96, local copies, waits for them, and re-layouts, memory_head(): lax.scan(jax.checkpoint(advance), (init_one, init_two, zero_state, zero_s...  114 us
    unnamed x1, blocking collectives  61.2 us
    unnamed x27, waiting for transfers between devices  60.6 us
    reduce_scatter x1, waiting for transfers between devices, on_device(): lax.psum_scatter(mix_grad.astype(jnp.bfloat16), 'fsdp', scatter_dimension...  58.9 us
    reduce_scatter x1, waiting for transfers between devices, on_device(): lax.psum_scatter(query_grad.astype(jnp.bfloat16), 'fsdp', scatter_dimensi...  58.8 us
    reduce_scatter x1, waiting for transfers between devices, on_device(): lax.psum_scatter(value_grad.astype(jnp.bfloat16), 'fsdp', scatter_dimensi...  58.8 us
    all_gather x1, waiting for transfers between devices, on_device(): lax.all_gather(down_weight, 'fsdp', axis=1, tiled=True)  46.1 us
  transfers between devices with their start and end apart: 26, of which 18 were waited for; matrix products, arithmetic and copies ran while one was open for 51% of the time, Pallas kernels for 0%

commit v1 on v0

v1 whole, which is shorter than its diff:
```python
import functools
import jax, jax.numpy as jnp
from jax import lax
from jax.experimental import pallas as pl
from jax.experimental.pallas import tpu as pltpu
from jax.sharding import PartitionSpec as P

HEAD = 128
SPAN = 64
SEQ_LEN = 1024
BF16 = jnp.bfloat16
F32 = jnp.float32
NN = (((1,), (0,)), ((), ()))
NT = (((1,), (1,)), ((), ()))
TN = (((0,), (0,)), ((), ()))


def dot(left, right, dims=NN):
    return lax.dot_general(left, right, dims, preferred_element_type=F32)


def sigmoid(values):
    return 0.5 * jnp.tanh(0.5 * values) + 0.5


def memory_forward_kernel(
    unroll, sequences, heads, starts_ref, rates_ref, queries_ref, keys_ref, values_ref, live_ref,
    init_ref, recalled_ref, states_ref, first_ref, second_ref, moment_one_ref, moment_two_ref,
):
    spans = SEQ_LEN // SPAN
    step = pl.program_id(0)
    chains = [(s, h) for s in range(sequences) for h in range(heads)]

    @pl.when(step == 0)
    def _():
        for place, (s, h) in enumerate(chains):
            first_ref[place] = jnp.zeros((HEAD, HEAD), F32)
            second_ref[place] = jnp.zeros((HEAD, HEAD), F32)
            moment_one_ref[place] = jnp.zeros((HEAD, HEAD), F32)
            moment_two_ref[place] = jnp.zeros((HEAD, HEAD), F32)

    state = [
        (first_ref[i], second_ref[i], moment_one_ref[i], moment_two_ref[i])
        for i in range(len(chains))
    ]
    for part in range(unroll):
        rows = pl.ds(part * SPAN, SPAN)
        span = step * unroll + part
        begins = [starts_ref[s * spans + span] != 0 for s in range(sequences)]
        used = []
        for place, (s, h) in enumerate(chains):
            one, two, moment_one, moment_two = state[place]
            start = init_ref[pl.ds(h * HEAD, HEAD), :]
            used.append(
                (
                    jnp.where(begins[s], start[:, :HEAD], one),
                    jnp.where(begins[s], start[:, HEAD:], two),
                    jnp.where(begins[s], 0.0, moment_one),
                    jnp.where(begins[s], 0.0, moment_two),
                )
            )
        low = [(one.astype(BF16), two.astype(BF16)) for one, two, _, _ in used]
        for place in range(len(chains)):
            states_ref[part, place, :, :HEAD] = low[place][0]
            states_ref[part, place, :, HEAD:] = low[place][1]
        cols = [pl.ds(h * HEAD, HEAD) for _, h in chains]
        keys = [keys_ref[s, rows, cols[i]] for i, (s, _) in enumerate(chains)]
        hidden = [dot(keys[i], low[i][0]) for i in range(len(chains))]
        gates = [sigmoid(value) for value in hidden]
        active = [(h * g).astype(BF16) for h, g in zip(hidden, gates)]
        outs = [dot(active[i], low[i][1]) for i in range(len(chains))]
        errors = [
            ((outs[i] - values_ref[s, rows, cols[i]].astype(F32)) * live_ref[s, rows, :]).astype(BF16)
            for i, (s, _) in enumerate(chains)
        ]
        back = [dot(errors[i], low[i][1], NT) for i in range(len(chains))]
        inner = [
            (b * (g * (1.0 + h * (1.0 - g)))).astype(BF16)
            for b, h, g in zip(back, hidden, gates)
        ]
        grad_one = [dot(keys[i], inner[i], TN) for i in range(len(chains))]
        grad_two = [dot(active[i], errors[i], TN) for i in range(len(chains))]
        state = []
        for place, (s, h) in enumerate(chains):
            one, two, moment_one, moment_two = used[place]
            index = (s * spans + span) * heads + h
            stride = sequences * spans * heads
            momentum = rates_ref[index]
            size = rates_ref[stride + index]
            keep = 1.0 - rates_ref[2 * stride + index]
            moment_one = momentum * moment_one - size * grad_one[place]
            moment_two = momentum * moment_two - size * grad_two[place]
            state.append((keep * one + moment_one, keep * two + moment_two, moment_one, moment_two))
        for place, (s, h) in enumerate(chains):
            asked = dot(queries_ref[s, rows, cols[place]], low[place][0])
            asked = (asked * sigmoid(asked)).astype(BF16)
            recalled_ref[s, rows, cols[place]] = dot(asked, low[place][1]).astype(recalled_ref.dtype)
    for place in range(len(chains)):
        first_ref[place], second_ref[place], moment_one_ref[place], moment_two_ref[place] = state[place]


def memory_forward(queries, key_rows, value_rows, live, starts, rates, init, unroll=2):
    rows, width = queries.shape
    sequences, heads = rows // SEQ_LEN, width // HEAD
    spans = SEQ_LEN // SPAN
    chains = sequences * heads

    def by_seq(values):
        return values.reshape(sequences, SEQ_LEN, width)

    block = pl.BlockSpec((sequences, unroll * SPAN, width), lambda c: (0, c, 0))
    smem = pl.BlockSpec(memory_space=pltpu.SMEM)
    recalled, states = pl.pallas_call(
        functools.partial(memory_forward_kernel, unroll, sequences, heads),
        grid=(spans // unroll,),
        in_specs=[
            smem, smem, block, block, block,
            pl.BlockSpec((sequences, unroll * SPAN, 1), lambda c: (0, c, 0)),
            pl.BlockSpec((heads * HEAD, 2 * HEAD), lambda c: (0, 0)),
        ],
        out_specs=[
            block,
            pl.BlockSpec((unroll, chains, HEAD, 2 * HEAD), lambda c: (c, 0, 0, 0)),
        ],
        out_shape=[
            jax.ShapeDtypeStruct((sequences, SEQ_LEN, width), F32),
            jax.ShapeDtypeStruct((spans, chains, HEAD, 2 * HEAD), BF16),
        ],
        scratch_shapes=[pltpu.VMEM((chains, HEAD, HEAD), F32)] * 4,
        name="memory_forward",
    )(
        starts, rates.reshape(-1), by_seq(queries), by_seq(key_rows), by_seq(value_rows),
        live.reshape(sequences, SEQ_LEN, 1), init,
    )
    return recalled.reshape(rows, width), states


def memory_backward_kernel(
    unroll, sequences, heads, starts_ref, rates_ref, queries_ref, keys_ref, values_ref, live_ref,
    grads_ref, states_ref, query_out, key_out, value_out, init_out,
    first_ref, second_ref, moment_one_ref, moment_two_ref, total_ref,
):
    spans = SEQ_LEN // SPAN
    step = pl.program_id(0)
    chains = [(s, h) for s in range(sequences) for h in range(heads)]
    count = len(chains)
    zero = jnp.zeros((HEAD, HEAD), F32)

    @pl.when(step == 0)
    def _():
        for i in range(count):
            first_ref[i] = zero
            second_ref[i] = zero
            moment_one_ref[i] = zero
            moment_two_ref[i] = zero
            total_ref[i] = jnp.zeros((HEAD, 2 * HEAD), F32)

    state = [(first_ref[i], second_ref[i], moment_one_ref[i], moment_two_ref[i]) for i in range(count)]
    cols = [pl.ds(h * HEAD, HEAD) for _, h in chains]
    for part in reversed(range(unroll)):
        rows = pl.ds(part * SPAN, SPAN)
        span = spans - (step + 1) * unroll + part
        stride = sequences * spans * heads
        each = range(count)
        one = [states_ref[part, i, :, :HEAD] for i in each]
        two = [states_ref[part, i, :, HEAD:] for i in each]
        queries = [queries_ref[chains[i][0], rows, cols[i]] for i in each]
        keys = [keys_ref[chains[i][0], rows, cols[i]] for i in each]
        values = [values_ref[chains[i][0], rows, cols[i]].astype(F32) for i in each]
        live = [live_ref[chains[i][0], rows, :] for i in each]
        grads = [grads_ref[chains[i][0], rows, cols[i]].astype(BF16) for i in each]
        hidden = [dot(keys[i], one[i]) for i in each]
        gates = [sigmoid(hidden[i]) for i in each]
        active = [(hidden[i] * gates[i]).astype(BF16) for i in each]
        errors = [((dot(active[i], two[i]) - values[i]) * live[i]).astype(BF16) for i in each]
        back = [dot(errors[i], two[i], NT) for i in each]
        slope = [gates[i] * (1.0 + hidden[i] * (1.0 - gates[i])) for i in each]
        bend = [
            gates[i] * (1.0 - gates[i]) * (2.0 + hidden[i] * (1.0 - 2.0 * gates[i])) * back[i]
            for i in each
        ]
        inner = [(back[i] * slope[i]).astype(BF16) for i in each]
        asked = [dot(queries[i], one[i]) for i in each]
        asked_gate = [sigmoid(asked[i]) for i in each]
        asked_active = [(asked[i] * asked_gate[i]).astype(BF16) for i in each]
        asked_grad = [
            (
                dot(grads[i], two[i], NT)
                * (asked_gate[i] * (1.0 + asked[i] * (1.0 - asked_gate[i])))
            ).astype(BF16)
            for i in each
        ]
        for i in each:
            query_out[chains[i][0], rows, cols[i]] = dot(asked_grad[i], one[i], NT)
        momentum, size, keep = [], [], []
        for s, h in chains:
            index = (s * spans + span) * heads + h
            momentum.append(rates_ref[index])
            size.append(rates_ref[stride + index])
            keep.append(1.0 - rates_ref[2 * stride + index])
        sum_one = [state[i][0] + state[i][2] for i in each]
        sum_two = [state[i][1] + state[i][3] for i in each]
        step_one = [(-size[i] * sum_one[i]).astype(BF16) for i in each]
        step_two = [(-size[i] * sum_two[i]).astype(BF16) for i in each]
        inner_grad = [dot(keys[i], step_one[i]) for i in each]
        back_grad = [(inner_grad[i] * slope[i]).astype(BF16) for i in each]
        error_grad = [
            (dot(back_grad[i], two[i]) + dot(active[i], step_two[i])) * live[i] for i in each
        ]
        for i in each:
            value_out[chains[i][0], rows, cols[i]] = -error_grad[i]
        out_grad = [error_grad[i].astype(BF16) for i in each]
        active_grad = [dot(errors[i], step_two[i], NT) + dot(out_grad[i], two[i], NT) for i in each]
        hidden_grad = [
            (active_grad[i] * slope[i] + inner_grad[i] * bend[i]).astype(BF16) for i in each
        ]
        new_one = [
            keep[i] * state[i][0] + dot(keys[i], hidden_grad[i], TN) + dot(queries[i], asked_grad[i], TN)
            for i in each
        ]
        new_two = [
            keep[i] * state[i][1]
            + dot(back_grad[i], errors[i], TN)
            + dot(active[i], out_grad[i], TN)
            + dot(asked_active[i], grads[i], TN)
            for i in each
        ]
        for i in each:
            key_out[chains[i][0], rows, cols[i]] = dot(inner[i], step_one[i], NT) + dot(
                hidden_grad[i], one[i], NT
            )
        begins = [starts_ref[s * spans + span] != 0 for s in range(sequences)]
        state = []
        for i, (s, h) in enumerate(chains):
            begin = begins[s]
            total_ref[i, :, :HEAD] += jnp.where(begin, new_one[i], 0.0)
            total_ref[i, :, HEAD:] += jnp.where(begin, new_two[i], 0.0)
            state.append(
                (
                    jnp.where(begin, 0.0, new_one[i]),
                    jnp.where(begin, 0.0, new_two[i]),
                    jnp.where(begin, 0.0, momentum[i] * sum_one[i]),
                    jnp.where(begin, 0.0, momentum[i] * sum_two[i]),
                )
            )
    for i in range(count):
        first_ref[i], second_ref[i], moment_one_ref[i], moment_two_ref[i] = state[i]

    @pl.when(step == pl.num_programs(0) - 1)
    def _():
        for h in range(heads):
            init_out[pl.ds(h * HEAD, HEAD), :] = sum(
                total_ref[s * heads + h] for s in range(sequences)
            )


def memory_backward(
    queries, key_rows, value_rows, live, starts, rates, grads, states, unroll=2
):
    rows, width = queries.shape
    sequences, heads = rows // SEQ_LEN, width // HEAD
    spans = SEQ_LEN // SPAN
    chains = sequences * heads
    steps = spans // unroll

    def by_seq(values):
        return values.reshape(sequences, SEQ_LEN, width)

    block = pl.BlockSpec((sequences, unroll * SPAN, width), lambda c: (0, steps - 1 - c, 0))
    smem = pl.BlockSpec(memory_space=pltpu.SMEM)
    shape = jax.ShapeDtypeStruct((sequences, SEQ_LEN, width), F32)
    query_mem, key_mem, value_mem, init_grad = pl.pallas_call(
        functools.partial(memory_backward_kernel, unroll, sequences, heads),
        grid=(steps,),
        in_specs=[
            smem, smem, block, block, block,
            pl.BlockSpec((sequences, unroll * SPAN, 1), lambda c: (0, steps - 1 - c, 0)),
            block,
            pl.BlockSpec((unroll, chains, HEAD, 2 * HEAD), lambda c: (steps - 1 - c, 0, 0, 0)),
        ],
        out_specs=[
            block, block, block,
            pl.BlockSpec((heads * HEAD, 2 * HEAD), lambda c: (0, 0)),
        ],
        out_shape=[
            shape, shape, shape,
            jax.ShapeDtypeStruct((heads * HEAD, 2 * HEAD), F32),
        ],
        scratch_shapes=[pltpu.VMEM((chains, HEAD, HEAD), F32)] * 4
        + [pltpu.VMEM((chains, HEAD, 2 * HEAD), F32)],
        name="memory_backward",
    )(
        starts, rates.reshape(-1), by_seq(queries), by_seq(key_rows), by_seq(value_rows),
        live.reshape(sequences, SEQ_LEN, 1), by_seq(grads), states,
    )
    return tuple(x.reshape(rows, width) for x in (query_mem, key_mem, value_mem)) + (init_grad,)

PERSIST = 16
TILE = 256
MASKED_SCORE = -1e30
SCALING = HEAD ** (-0.5)


def masked_scores(tile, queries, keys_ref, column_ref, row_ref):
    reach = (tile + 1) * TILE
    scores = dot(keys_ref[0, :reach, :], queries, NT) * SCALING
    same = column_ref[0, :reach, :] == row_ref[0, :, tile * TILE : reach]
    if tile:
        early = jnp.where(same[: tile * TILE], scores[: tile * TILE], MASKED_SCORE)
    own = same[tile * TILE :] & (
        lax.broadcasted_iota(jnp.int32, (TILE, TILE), 0)
        <= lax.broadcasted_iota(jnp.int32, (TILE, TILE), 1)
    )
    own = jnp.where(own, scores[tile * TILE :], MASKED_SCORE)
    return jnp.concatenate([early, own], axis=0) if tile else own


def attention_forward_kernel(
    queries_ref, keys_ref, values_ref, persist_ref, column_ref, row_ref, gate_ref, recalled_ref,
    combined_ref, log_ref,
):
    values_t = values_ref[0].T
    fixed_keys = persist_ref[:PERSIST, :]
    fixed_values_t = persist_ref[PERSIST:, :].astype(F32).T.astype(BF16)
    for tile in range(SEQ_LEN // TILE):
        rows = slice(tile * TILE, (tile + 1) * TILE)
        reach = (tile + 1) * TILE
        queries = queries_ref[0, rows, :]
        scores = masked_scores(tile, queries, keys_ref, column_ref, row_ref)
        fixed = dot(fixed_keys, queries, NT) * SCALING
        highest = jnp.maximum(
            jnp.max(scores, axis=0, keepdims=True), jnp.max(fixed, axis=0, keepdims=True)
        )
        weights = jnp.exp(scores - highest)
        fixed_weights = jnp.exp(fixed - highest)
        totals = jnp.sum(weights, axis=0, keepdims=True) + jnp.sum(
            fixed_weights, axis=0, keepdims=True
        )
        part = 1.0 / totals
        attended = dot(values_t[:, :reach], (weights * part).astype(BF16)) + dot(
            fixed_values_t, (fixed_weights * part).astype(BF16)
        )
        log_ref[0, 0, :, rows] = highest + jnp.log(totals)
        combined_ref[0, rows, :] = (
            attended.T + sigmoid(gate_ref[0, rows, :]) * recalled_ref[0, rows, :]
        ).astype(BF16)


def attention_forward(queries, key_rows, value_rows, persist, documents, gate_pre, recalled):
    rows, width = queries.shape
    sequences, heads = rows // SEQ_LEN, width // HEAD

    def by_seq(values):
        return values.reshape(sequences, SEQ_LEN, width)

    block = pl.BlockSpec((1, SEQ_LEN, HEAD), lambda h, s: (s, 0, h))
    combined, logs = pl.pallas_call(
        attention_forward_kernel,
        grid=(heads, sequences),
        in_specs=[
            block, block, block,
            pl.BlockSpec((2 * PERSIST, HEAD), lambda h, s: (0, h)),
            pl.BlockSpec((1, SEQ_LEN, 1), lambda h, s: (s, 0, 0)),
            pl.BlockSpec((1, 1, SEQ_LEN), lambda h, s: (s, 0, 0)),
            block, block,
        ],
        out_specs=[block, pl.BlockSpec((1, 1, 1, SEQ_LEN), lambda h, s: (s, h, 0, 0))],
        out_shape=[
            jax.ShapeDtypeStruct((sequences, SEQ_LEN, width), BF16),
            jax.ShapeDtypeStruct((sequences, heads, 1, SEQ_LEN), F32),
        ],
        name="attention_forward",
    )(
        by_seq(queries), by_seq(key_rows), by_seq(value_rows), persist,
        documents.reshape(sequences, SEQ_LEN, 1), documents.reshape(sequences, 1, SEQ_LEN),
        by_seq(gate_pre), by_seq(recalled),
    )
    return combined.reshape(rows, width), logs


def attention_backward_kernel(
    queries_ref, keys_ref, values_ref, persist_ref, column_ref, row_ref, log_ref, grad_ref,
    query_mem_ref, key_mem_ref, value_mem_ref,
    query_out, key_out, value_out, persist_out, key_total, value_total,
):
    keys_t = keys_ref[0].T
    fixed_keys = persist_ref[:PERSIST, :]
    fixed_values = persist_ref[PERSIST:, :]
    fixed_keys_t = fixed_keys.astype(F32).T.astype(BF16)

    @pl.when(pl.program_id(1) == 0)
    def _():
        persist_out[...] = jnp.zeros(persist_out.shape, F32)

    for tile in reversed(range(SEQ_LEN // TILE)):
        rows = slice(tile * TILE, (tile + 1) * TILE)
        reach = (tile + 1) * TILE
        queries = queries_ref[0, rows, :]
        grads = grad_ref[0, rows, :]
        logs = log_ref[0, 0, :, rows]
        scores = masked_scores(tile, queries, keys_ref, column_ref, row_ref)
        prob = jnp.exp(scores - logs)
        fixed_prob = jnp.exp(dot(fixed_keys, queries, NT) * SCALING - logs)
        prob_grad = dot(values_ref[0, :reach, :], grads, NT)
        fixed_prob_grad = dot(fixed_values, grads, NT)
        inner = jnp.sum(prob * prob_grad, axis=0, keepdims=True) + jnp.sum(
            fixed_prob * fixed_prob_grad, axis=0, keepdims=True
        )
        score_grad = (prob * (prob_grad - inner)).astype(BF16)
        fixed_score_grad = (fixed_prob * (fixed_prob_grad - inner)).astype(BF16)
        key_part = dot(score_grad, queries)
        value_part = dot(prob.astype(BF16), grads)
        if tile == SEQ_LEN // TILE - 1:
            key_total[...] = key_part
            value_total[...] = value_part
        else:
            key_total[:reach, :] += key_part
            value_total[:reach, :] += value_part
        persist_out[:PERSIST, :] += SCALING * dot(fixed_score_grad, queries)
        persist_out[PERSIST:, :] += dot(fixed_prob.astype(BF16), grads)
        query_part = dot(keys_t[:, :reach], score_grad) + dot(fixed_keys_t, fixed_score_grad)
        query_out[0, rows, :] = (SCALING * query_part.T + query_mem_ref[0, rows, :]).astype(BF16)
    key_out[0] = (SCALING * key_total[...] + key_mem_ref[0]).astype(BF16)
    value_out[0] = (value_total[...] + value_mem_ref[0]).astype(BF16)


def attention_backward(
    queries, key_rows, value_rows, persist, documents, logs, attended_grad,
    query_mem, key_mem, value_mem,
):
    rows, width = queries.shape
    sequences, heads = rows // SEQ_LEN, width // HEAD

    def by_seq(values):
        return values.reshape(sequences, SEQ_LEN, width)

    block = pl.BlockSpec((1, SEQ_LEN, HEAD), lambda h, s: (s, 0, h))
    fixed = pl.BlockSpec((2 * PERSIST, HEAD), lambda h, s: (0, h))
    shape = jax.ShapeDtypeStruct((sequences, SEQ_LEN, width), BF16)
    query_back, key_back, value_back, persist_grad = pl.pallas_call(
        attention_backward_kernel,
        grid=(heads, sequences),
        in_specs=[
            block, block, block, fixed,
            pl.BlockSpec((1, SEQ_LEN, 1), lambda h, s: (s, 0, 0)),
            pl.BlockSpec((1, 1, SEQ_LEN), lambda h, s: (s, 0, 0)),
            pl.BlockSpec((1, 1, 1, SEQ_LEN), lambda h, s: (s, h, 0, 0)),
            block, block, block, block,
        ],
        out_specs=[block, block, block, fixed],
        out_shape=[shape, shape, shape, jax.ShapeDtypeStruct((2 * PERSIST, width), F32)],
        scratch_shapes=[pltpu.VMEM((SEQ_LEN, HEAD), F32)] * 2,
        name="attention_backward",
    )(
        by_seq(queries), by_seq(key_rows), by_seq(value_rows), persist,
        documents.reshape(sequences, SEQ_LEN, 1), documents.reshape(sequences, 1, SEQ_LEN),
        logs, by_seq(attended_grad), by_seq(query_mem), by_seq(key_mem), by_seq(value_mem),
    )
    return tuple(x.reshape(rows, width) for x in (query_back, key_back, value_back)) + (persist_grad,)


EPSILON = 1e-05


def turn(left, right):
    return lax.dot_general(left, right, TN, preferred_element_type=F32)


def matmul(left, right):
    return lax.dot_general(left, right, NN, preferred_element_type=F32)


def matmul_right(left, right):
    return lax.dot_general(left, right, NT, preferred_element_type=F32)


def rms_norm(values, gain):
    return values * lax.rsqrt(jnp.mean(values * values, axis=-1, keepdims=True) + EPSILON) * gain


def norm_back(values, gain, grads):
    scale = lax.rsqrt(jnp.mean(values * values, axis=-1, keepdims=True) + EPSILON)
    weighted = grads * gain
    inner = jnp.mean(values * weighted, axis=-1, keepdims=True)
    return scale * weighted - values * (scale * scale * scale * inner), jnp.sum(
        grads * values * scale, axis=0
    )


class Group:
    def __init__(self):
        self.size = lax.axis_size("tp")
        self.rank = lax.axis_index("tp")

    def swap(self, values):
        return lax.ppermute(values, "tp", [(0, 1), (1, 0)])

    def spread(self, own):
        if self.size == 2:
            return [own, self.swap(own)]
        return [lax.all_gather(own, "tp", axis=0, tiled=True)]

    def collect(self, chunks):
        if self.size == 2:
            other = self.swap(chunks[1].astype(BF16))
            return chunks[0] + other.astype(F32)
        return lax.psum_scatter(
            chunks[0].astype(BF16), "tp", scatter_dimension=0, tiled=True
        ).astype(F32)

    def ordered(self, chunks):
        if self.size == 2:
            own, other = chunks
            first = self.rank == 0
            return jnp.concatenate(
                [jnp.where(first, own, other), jnp.where(first, other, own)], axis=0
            )
        return chunks[0]

    def chunks(self, rows):
        if self.size == 2:
            half = rows.shape[0] // 2
            return [
                lax.dynamic_slice_in_dim(rows, self.rank * half, half),
                lax.dynamic_slice_in_dim(rows, (1 - self.rank) * half, half),
            ]
        return [rows]


def gather_packed(parts):
    local = parts[0].shape[0]
    flat = [part.reshape(local, -1) for part in parts]
    widths = [part.shape[1] for part in flat]
    spare = -sum(widths) % 128
    if spare:
        flat.append(jnp.zeros((local, spare), flat[0].dtype))
    whole = lax.all_gather(jnp.concatenate(flat, axis=1), "fsdp", axis=0, tiled=True)
    outs, at = [], 0
    for width in widths:
        outs.append(whole[:, at : at + width])
        at += width
    return outs


def scatter_packed(parts, local):
    widths = [part.shape[1] for part in parts]
    flat = [part.astype(BF16) for part in parts]
    spare = -sum(widths) % 128
    if spare:
        flat.append(jnp.zeros((flat[0].shape[0], spare), BF16))
    total = lax.psum_scatter(
        jnp.concatenate(flat, axis=1), "fsdp", scatter_dimension=0, tiled=True
    ).astype(F32)
    outs, at = [], 0
    for width in widths:
        outs.append(total[:, at : at + width])
        at += width
    return outs


def on_device(
    tokens,
    norm_gains,
    query_weight,
    key_weight,
    value_weight,
    mix_gate_weight,
    output_weight,
    persistent_tokens,
    memory_init,
    gate_weight,
    up_weight,
    down_weight,
    doc_ids,
    span_starts,
    memory_rates,
    out_grad,
):
    group = Group()
    fsdp = lax.axis_size("fsdp")
    local = query_weight.shape[0]
    width = query_weight.shape[1]
    shares = fsdp * local
    token_chunks = group.spread(tokens)
    grad_chunks = group.spread(out_grad)
    w_query, w_key, w_value, w_mix, packed_init, packed_persist, packed_gains = gather_packed(
        [
            query_weight,
            key_weight,
            value_weight,
            mix_gate_weight,
            memory_init.T.reshape(local, -1),
            persistent_tokens.reshape(local, -1),
            norm_gains.T,
        ]
    )
    w_out, w_gate, w_up, w_down = gather_packed(
        [output_weight.T, gate_weight, up_weight, down_weight.T]
    )
    init = packed_init.reshape(2 * HEAD, width).T.astype(F32)
    persist = packed_persist.reshape(2 * PERSIST, width)
    gains = packed_gains.T.astype(F32)

    rows_in = tokens.astype(F32)
    normed_all = group.ordered(
        [rms_norm(chunk.astype(F32), gains[0]).astype(BF16) for chunk in token_chunks]
    )
    queries = matmul(normed_all, w_query).astype(BF16)
    key_rows = matmul(normed_all, w_key).astype(BF16)
    value_rows = matmul(normed_all, w_value).astype(BF16)
    gate_pre = matmul(normed_all, w_mix)
    doc_blocks = doc_ids.reshape(-1, SPAN)
    live = (doc_blocks == doc_blocks[:, SPAN - 1 :]).astype(F32) / SPAN
    recalled, states = memory_forward(
        queries, key_rows, value_rows, live, span_starts, memory_rates, init
    )
    combined, logs = attention_forward(
        queries, key_rows, value_rows, persist, doc_ids, gate_pre, recalled
    )
    branch = group.collect([matmul_right(chunk, w_out) for chunk in group.chunks(combined)])
    hidden_one = rows_in + branch
    normed_two = rms_norm(hidden_one, gains[1]).astype(BF16)
    normed_chunks = group.spread(normed_two)

    ffn, back_chunks, gate_backs, up_backs, hiddens = [], [], [], [], []
    for rows, grads in zip(normed_chunks, grad_chunks):
        gate_rows = matmul(rows, w_gate)
        up_rows = matmul(rows, w_up)
        gate_sigmoid = jax.nn.sigmoid(gate_rows)
        hidden = (gate_rows * gate_sigmoid * up_rows).astype(BF16)
        hidden_grad = matmul(grads, w_down)
        gate_back = (
            hidden_grad * up_rows * gate_sigmoid * (1.0 + gate_rows * (1.0 - gate_sigmoid))
        ).astype(BF16)
        up_back = (hidden_grad * gate_rows * gate_sigmoid).astype(BF16)
        ffn.append(matmul_right(hidden, w_down))
        back_chunks.append(matmul_right(gate_back, w_gate) + matmul_right(up_back, w_up))
        hiddens.append(hidden)
        gate_backs.append(gate_back)
        up_backs.append(up_back)
    output = (hidden_one + group.collect(ffn)).astype(BF16)
    normed_two_grad = group.collect(back_chunks)
    inner_grad, gain_two_grad = norm_back(hidden_one, gains[1], normed_two_grad)
    hidden_one_grad = out_grad.astype(F32) + inner_grad
    branch_rows = group.ordered(group.spread(hidden_one_grad.astype(BF16)))

    normed_two_all = jnp.concatenate(normed_chunks, axis=0)
    hidden_all = jnp.concatenate(hiddens, axis=0)
    down_grad = turn(jnp.concatenate(grad_chunks, axis=0), hidden_all)
    gate_grad = turn(normed_two_all, jnp.concatenate(gate_backs, axis=0))
    up_grad = turn(normed_two_all, jnp.concatenate(up_backs, axis=0))
    out_weight_grad = turn(branch_rows, combined)
    combined_grad = matmul(branch_rows, w_out)
    out_weight_out, gate_out, up_out, down_out = scatter_packed(
        [out_weight_grad, gate_grad, up_grad, down_grad], local
    )

    attended_grad = combined_grad.astype(BF16)
    gate_open = jax.nn.sigmoid(gate_pre)
    gate_pre_grad = (combined_grad * recalled * gate_open * (1.0 - gate_open)).astype(BF16)
    recalled_grad = combined_grad * gate_open
    query_mem, key_mem, value_mem, init_grad = memory_backward(
        queries, key_rows, value_rows, live, span_starts, memory_rates, recalled_grad, states
    )
    query_back, key_back, value_back, persist_grad = attention_backward(
        queries, key_rows, value_rows, persist, doc_ids, logs, attended_grad,
        query_mem, key_mem, value_mem,
    )
    backs = [query_back, key_back, value_back, gate_pre_grad]
    weights = [w_query, w_key, w_value, w_mix]
    pieces = [group.chunks(back) for back in backs]
    normed_grad = group.collect(
        [
            sum(matmul_right(piece[i], weight) for piece, weight in zip(pieces, weights))
            for i in range(len(pieces[0]))
        ]
    )
    query_out, key_out, value_out, mix_out, init_out, persist_out = scatter_packed(
        [turn(normed_all, back) for back in backs]
        + [init_grad.T.reshape(shares, -1), persist_grad.reshape(shares, -1)],
        local,
    )
    input_grad, gain_one_grad = norm_back(rows_in, gains[0], normed_grad)
    tokens_grad = (hidden_one_grad + input_grad).astype(BF16)
    gain_terms = jnp.stack([gain_one_grad, gain_two_grad]).reshape(2, fsdp, local)
    gain_terms = lax.all_to_all(gain_terms.transpose(1, 0, 2), "fsdp", 0, 0, tiled=True)
    gains_grad = lax.psum(jnp.sum(gain_terms, axis=0), "tp")
    return (
        output,
        tokens_grad,
        gains_grad,
        query_out,
        key_out,
        value_out,
        mix_out,
        out_weight_out.T,
        persist_out.reshape(persistent_tokens.shape),
        init_out.reshape(-1, width).T,
        gate_out,
        up_out,
        down_out.T,
    )


def solution(mesh):
    placed = (
        P(("fsdp", "tp"), None),
        P(None, "fsdp"),
        P("fsdp", "tp"),
        P("fsdp", "tp"),
        P("fsdp", "tp"),
        P("fsdp", "tp"),
        P("tp", "fsdp"),
        P("fsdp", "tp"),
        P("tp", "fsdp"),
        P("fsdp", "tp"),
        P("fsdp", "tp"),
        P("tp", "fsdp"),
        P("fsdp"),
        P("fsdp"),
        P(None, "fsdp", "tp"),
        P(("fsdp", "tp"), None),
    )
    return jax.shard_map(
        on_device,
        mesh=mesh,
        in_specs=placed,
        out_specs=(
            P(("fsdp", "tp"), None),
            P(("fsdp", "tp"), None),
            P(None, "fsdp"),
            P("fsdp", "tp"),
            P("fsdp", "tp"),
            P("fsdp", "tp"),
            P("fsdp", "tp"),
            P("tp", "fsdp"),
            P("fsdp", "tp"),
            P("tp", "fsdp"),
            P("fsdp", "tp"),
            P("fsdp", "tp"),
            P("tp", "fsdp"),
        ),
        check_vma=False,
    )
```

time: 1730 us -> 564 us (0.33)
  matrix products: 511 us -> 110 us
  waiting for transfers between devices: 647 us -> 284 us
  local copies, waits for them, and re-layouts: 226 us -> 35.9 us
  other arithmetic: 182 us -> 24.5 us
  blocking collectives: 127 us -> 5.48 us
  Pallas kernels: 0 us -> 67.9 us
    dot_general x436 -> x35, matrix products: 511 us -> 110 us  [the longest x16 41.3 us: matmul_right(): return lax.dot_general(left, right, NT, preferred_element_type=F32)]
    reduce_scatter x13 -> x1, waiting for transfers between devices: 338 us -> 80.8 us  [scatter_packed(): lax.psum_scatter(jnp.concatenate(flat, axis=1), 'fsdp', scatter_dimension...]
    all_gather x12 -> x2, waiting for transfers between devices: 249 us -> 66.3 us  [gather_packed(): lax.all_gather(jnp.concatenate(flat, axis=1), 'fsdp', axis=0, tiled=True)]
    ppermute x0 -> x8, waiting for transfers between devices: none -> 136 us  [swap(): return lax.ppermute(values, 'tp', [(0, 1), (1, 0)])]
    squeeze x96 -> x0, local copies, waits for them, and re-layouts: 114 us -> none  [memory_head(): lax.scan(jax.checkpoint(advance), (init_one, init_two, zero_state, zero_s...]
    pallas_call x0 -> x4, Pallas kernels: none -> 67.9 us  [the longest x1 26.8 us: memory_backward(): pl.pallas_call(functools.partial(memory_backward_kernel, unroll, sequence...]
    unnamed x1 -> x0, blocking collectives: 61.2 us -> none
    unnamed x27 -> x5, waiting for transfers between devices: 60.6 us -> 0.07 us
  transfers between devices with their start and end apart: 26 -> 13, of which waited for: 18 -> 12; matrix products, arithmetic and copies ran while one was open for 51% -> 21% of each run, Pallas kernels for 0% -> 5%
where the time goes in v1:
time: 564 us; the launch traced here: 558 us
  waiting for transfers between devices  284 us (50%)
  matrix products  110 us (20%)
  Pallas kernels  67.9 us (12%)
  local copies, waits for them, and re-layouts  35.9 us (6%)
  other arithmetic  24.5 us (4%)
  starting transfers between devices  15.5 us (3%)
  between operations  14.6 us (3%)
    ppermute x8, waiting for transfers between devices, swap(): return lax.ppermute(values, 'tp', [(0, 1), (1, 0)])  136 us
    reduce_scatter x1, waiting for transfers between devices, scatter_packed(): lax.psum_scatter(jnp.concatenate(flat, axis=1), 'fsdp', scatter_dimension...  80.8 us
    all_gather x2, waiting for transfers between devices, gather_packed(): lax.all_gather(jnp.concatenate(flat, axis=1), 'fsdp', axis=0, tiled=True)  66.3 us
    dot_general x16, matrix products, matmul_right(): return lax.dot_general(left, right, NT, preferred_element_type=F32)  41.3 us
    dot_general x8, matrix products, turn(): return lax.dot_general(left, right, TN, preferred_element_type=F32)  34.9 us
    dot_general x11, matrix products, matmul(): return lax.dot_general(left, right, NN, preferred_element_type=F32)  33.7 us
    pallas_call x1, Pallas kernels, memory_backward(): pl.pallas_call(functools.partial(memory_backward_kernel, unroll, sequence...  26.8 us
    unnamed x100, local copies, waits for them, and re-layouts  15.9 us
  transfers between devices with their start and end apart: 13, of which 12 were waited for; matrix products, arithmetic and copies ran while one was open for 21% of the time, Pallas kernels for 5%

profile of v1, /device:TPU:0, one launch (start us, length us, event | category | flops | bytes accessed | tf_op | source)
XLA Modules:
  0.0 558.2 jit_solution(16179573641958201938)
XLA Ops:
  13.5 3.0 collective-permute-start
  20.1 19.6 %collective-permute-done = bf16[512,1024]{1,0:T(8,128)(2,1)S(1)} collective-permute-done((bf16[512,1024]{1,0:T(8,128)(2,1)S(1)}, bf16[512,1024]{1,0:T(8,128)(2,1)S(1)}, u32[]{:S(2)}, u32[]{:S(2)}) %collective-permute-start) | collective-permute-done | bytes 1048608 | tf_op jit(solution)/shard_map/ppermute | solution.py:496
  40.0 27.4 %all-gather.3.cloned.1.call-done = bf16[1024,2304]{1,0:T(8,128)(2,1)} async-done(((bf16[64,2304]{1,0:T(8,128)(2,1)}), bf16[1024,2304]{1,0:T(8,128)(2,1)}) %all-gather.3.cloned.1.call-update) | async-done | bytes 4718608 | tf_op jit(solution)/shard_map/all_gather | solution.py:537
  75.3 2.2 fusion.60.queries_ref
  77.5 2.2 fusion.61.keys_ref
  79.8 2.2 fusion.62.values_ref
  82.0 13.8 %memory_forward.1 = (f32[1,1024,512]{2,1,0:T(8,128)}, bf16[16,4,128,256]{3,2,1,0:T(8,128)(2,1)}) custom-call(s32[16]{0:T(128)} %starts_ref.3, f32[192]{0:T(256)} %reshape.184.rates_ref, bf16[1,1024,512]{2,1,0:T(8,128)(2,1)} %fusion.60.queries_ref, bf16[1,1024,512]{2,1,0:T(8,128)(2,1)} %fusion.61.keys_ref, bf16[1,1024,512]{2,1,0:T(8,128)(2,1)} %fusion.62.values_ref, ...), custom_call_target="tpu_custom_call" | custom-call | tf_op jit(solution)/shard_map/memory_forward/pallas_call | solution.py:113
  95.8 3.8 fusion.78
  99.6 12.2 %attention_forward.1 = (bf16[1,1024,512]{2,1,0:T(8,128)(2,1)}, f32[1,4,1,1024]{3,2,1,0:T(1,128)}) custom-call(bf16[1,1024,512]{2,1,0:T(8,128)(2,1)} %fusion.60.queries_ref, bf16[1,1024,512]{2,1,0:T(8,128)(2,1)} %fusion.61.keys_ref, bf16[1,1024,512]{2,1,0:T(8,128)(2,1)} %fusion.62.values_ref, bf16[32,512]{1,0:T(8,128)(2,1)} %reshape.180.persist_ref, ...), custom_call_target="tpu_custom_call" | custom-call | tf_op jit(solution)/shard_map/attention_forward/pallas_call | solution.py:357
  111.8 38.9 %all-gather.5.cloned.1.call-done = bf16[1024,4736]{1,0:T(8,128)(2,1)} async-done(((bf16[64,4736]{1,0:T(8,128)(2,1)}), bf16[1024,4736]{1,0:T(8,128)(2,1)}) %all-gather.5.cloned.1.call-update) | async-done | bytes 9699344 | tf_op jit(solution)/shard_map/all_gather | solution.py:537
  150.8 2.1 convolution_convert_fusion.11
  155.0 24.1 %collective-permute-done.1 = bf16[512,1024]{1,0:T(8,128)(2,1)} collective-permute-done((bf16[512,1024]{1,0:T(8,128)(2,1)S(1)}, bf16[512,1024]{1,0:T(8,128)(2,1)}, u32[]{:S(2)}, u32[]{:S(2)}) %collective-permute-start.1) | collective-permute-done | bytes 1048608 | tf_op jit(solution)/shard_map/ppermute | solution.py:496
  179.1 2.7 multiply_reduce_fusion.2
  183.6 4.7 convolution_bitcast_fusion.1
  188.2 13.3 %collective-permute-done.4 = bf16[512,1024]{1,0:T(8,128)(2,1)} collective-permute-done((bf16[512,1024]{1,0:T(8,128)(2,1)}, bf16[512,1024]{1,0:T(8,128)(2,1)}, u32[]{:S(2)}, u32[]{:S(2)}) %collective-permute-start.4) | collective-permute-done | bytes 1048608 | tf_op jit(solution)/shard_map/ppermute | solution.py:496
  201.6 3.0 convolution_bitcast_fusion
  206.4 16.8 %collective-permute-done.2 = bf16[512,1024]{1,0:T(8,128)(2,1)S(1)} collective-permute-done((bf16[512,1024]{1,0:T(8,128)(2,1)S(1)}, bf16[512,1024]{1,0:T(8,128)(2,1)S(1)}, u32[]{:S(2)}, u32[]{:S(2)}) %collective-permute-start.2) | collective-permute-done | bytes 1048608 | tf_op jit(solution)/shard_map/ppermute | solution.py:496
  225.0 4.2 multiply_convert_fusion.1
  234.5 4.0 multiply_convert_fusion.3
  240.3 17.2 %collective-permute-done.5 = bf16[512,1024]{1,0:T(8,128)(2,1)S(1)} collective-permute-done((bf16[512,1024]{1,0:T(8,128)(2,1)S(1)}, bf16[512,1024]{1,0:T(8,128)(2,1)S(1)}, u32[]{:S(2)}, u32[]{:S(2)}) %collective-permute-start.5) | collective-permute-done | bytes 1048608 | tf_op jit(solution)/shard_map/ppermute | solution.py:496
  257.5 2.3 multiply_reduce_fusion
  259.8 2.5 fusion.130
  263.8 22.1 %collective-permute-done.6 = bf16[512,1024]{1,0:T(8,128)(2,1)S(1)} collective-permute-done((bf16[512,1024]{1,0:T(8,128)(2,1)S(1)}, bf16[512,1024]{1,0:T(8,128)(2,1)S(1)}, u32[]{:S(2)}, u32[]{:S(2)}) %collective-permute-start.6) | collective-permute-done | bytes 1048608 | tf_op jit(solution)/shard_map/ppermute | solution.py:496
  286.2 3.7 fusion.26
  290.0 26.8 %memory_backward.1 = (f32[1,1024,512]{2,1,0:T(8,128)}, f32[1,1024,512]{2,1,0:T(8,128)}, f32[1,1024,512]{2,1,0:T(8,128)}, f32[512,256]{1,0:T(8,128)}) custom-call(s32[16]{0:T(128)} %starts_ref.3, f32[192]{0:T(256)} %reshape.184.rates_ref, bf16[1,1024,512]{2,1,0:T(8,128)(2,1)} %fusion.60.queries_ref, bf16[1,1024,512]{2,1,0:T(8,128)(2,1)} %fusion.61.keys_ref, ...), custom_call_target="tpu_custom_call" | custom-call | tf_op jit(solution)/shard_map/memory_backward/pallas_call | solution.py:272
  316.8 15.1 %attention_backward.1 = (bf16[1,1024,512]{2,1,0:T(8,128)(2,1)}, bf16[1,1024,512]{2,1,0:T(8,128)(2,1)}, bf16[1,1024,512]{2,1,0:T(8,128)(2,1)}, f32[32,512]{1,0:T(8,128)}) custom-call(bf16[1,1024,512]{2,1,0:T(8,128)(2,1)} %fusion.60.queries_ref, bf16[1,1024,512]{2,1,0:T(8,128)(2,1)} %fusion.61.keys_ref, bf16[1,1024,512]{2,1,0:T(8,128)(2,1)} %fusion.62.values_ref, ...), custom_call_target="tpu_custom_call" | custom-call | tf_op jit(solution)/shard_map/attention_backward/pallas_call | solution.py:440
  331.9 4.2 fusion.55
  339.3 4.2 fusion.54
  343.5 2.3 fusion.53
  345.9 2.3 fusion.52
  350.2 6.8 %copy.87 = bf16[1024,2304]{1,0:T(8,128)(2,1)} copy(bf16[1024,2304]{0,1:T(8,128)(2,1)} %broadcast_dynamic-update-slice_fusion) | data formatting | bytes 9437184
  357.1 7.6 %convolution_convert_fusion.1 = bf16[1024,1408]{1,0:T(8,128)(2,1)} fusion(bf16[512,1408]{1,0:T(8,128)(2,1)} %copy-done.37, bf16[512,1408]{1,0:T(8,128)(2,1)} %copy-done.38, bf16[512,1024]{1,0:T(8,128)(2,1)} %copy-done.33, bf16[512,1024]{1,0:T(8,128)(2,1)} %copy-done.18), kind=kOutput, calls=%fused_computation.8 | convolution fusion | flops 2964193280 | bytes 7864320 | tf_op jit(solution)/shard_map/dot_general | solution.py:466
  364.8 5.1 convolution_convert_fusion.2
  369.9 6.8 %convolution_convert_fusion = bf16[1024,1408]{1,0:T(8,128)(2,1)} fusion(bf16[512,1408]{1,0:T(8,128)(2,1)S(1)} %copy-done.39, bf16[512,1408]{1,0:T(8,128)(2,1)S(1)} %copy-done.40, bf16[512,1024]{1,0:T(8,128)(2,1)} %collective-permute-done.4, bf16[512,1024]{1,0:T(8,128)(2,1)} %param.31), kind=kOutput, calls=%fused_computation.7 | convolution fusion | flops 2964193280 | bytes 7864320 | tf_op jit(solution)/shard_map/dot_general | solution.py:466
  376.7 2.3 convolution_convert_fusion.3
  379.0 2.3 copy.80
  381.3 9.2 %pad_maximum_fusion = bf16[1024,4736]{1,0:T(8,128)(2,1)} fusion(bf16[1024,1408]{1,0:T(8,128)(2,1)} %convolution_convert_fusion, bf16[1024,1408]{1,0:T(8,128)(2,1)} %convolution_convert_fusion.1, bf16[1024,1408]{1,0:T(8,128)(2,1)} %convolution_convert_fusion.2, bf16[1024,512]{1,0:T(8,128)(2,1)} %copy.80), kind=kLoop, calls=%fused_computation | loop fusion | flops 38797312 | bytes 19398656 | tf_op jit(solution)/shard_map/concatenate | solution.py:552
  390.5 4.2 fusion.49
  402.3 3.1 add_convert_fusion
  406.1 14.7 %collective-permute-done.3 = bf16[512,1024]{1,0:T(8,128)(2,1)S(1)} collective-permute-done((bf16[512,1024]{1,0:T(8,128)(2,1)S(1)}, bf16[512,1024]{1,0:T(8,128)(2,1)S(1)}, u32[]{:S(2)}, u32[]{:S(2)}) %collective-permute-start.3) | collective-permute-done | bytes 1048608 | tf_op jit(solution)/shard_map/ppermute | solution.py:496
  420.8 4.7 add_convert_fusion.2
  425.6 2.2 fusion.82
  432.0 8.1 %collective-permute-done.7 = bf16[512,1024]{1,0:T(8,128)(2,1)} collective-permute-done((bf16[512,1024]{1,0:T(8,128)(2,1)}, bf16[512,1024]{1,0:T(8,128)(2,1)}, u32[]{:S(2)}, u32[]{:S(2)}) %collective-permute-start.7) | collective-permute-done | bytes 1048608 | tf_op jit(solution)/shard_map/ppermute | solution.py:496
  440.0 4.4 fusion.20
  445.2 3.5 all-to-all-start
  448.7 5.0 fusion.18
  456.4 5.5 psum.7
  467.8 80.8 %reduce-scatter.5.cloned.1.call-done = bf16[64,4736]{1,0:T(8,128)(2,1)} async-done(((bf16[1024,4736]{1,0:T(8,128)(2,1)}), bf16[64,4736]{1,0:T(8,128)(2,1)}) %reduce-scatter.5.cloned.1.call-update) | async-done | bytes 606224 | tf_op jit(solution)/shard_map/reduce_scatter | solution.py:551
  (180 shorter events, 64.3 us)
Async XLA Ops:
  7.2 6.3 %copy-start.1 = (bf16[512,1024]{1,0:T(8,128)(2,1)S(1)}, bf16[512,1024]{1,0:T(8,128)(2,1)}, u32[]{:S(2)}) copy-start(bf16[512,1024]{1,0:T(8,128)(2,1)} %param.16) | copy-start | bytes 3145732
  7.2 9.4 %copy-start.28 = (s32[1024]{0:T(1024)S(1)}, s32[1024]{0:T(1024)}, u32[]{:S(2)}) copy-start(s32[1024]{0:T(1024)} %param.28) | copy-start | bytes 12292
  7.2 10.5 %copy-start.30 = (f32[3,16,4]{1,2,0:T(4,128)S(1)}, f32[3,16,4]{1,2,0:T(4,128)}, u32[]{:S(2)}) copy-start(f32[3,16,4]{1,2,0:T(4,128)} %param.30) | copy-start | bytes 2308
  7.2 60.2 %all-gather.3.cloned.1.call-start = ((), (), s32[]{:S(2)}) async-start(), calls=%async_computation.3 | async-start | bytes 5013504 | tf_op jit(solution)/shard_map/all_gather | solution.py:537
  11.4 139.4 %all-gather.5.cloned.1.call-start = ((), (), s32[]{:S(2)}) async-start(), calls=%async_computation.4 | async-start | bytes 10305536 | tf_op jit(solution)/shard_map/all_gather | solution.py:537
  13.5 448.4 %reduce-scatter.7.cloned.1.call-start = ((), (), s32[]{:S(2)}) async-start(), calls=%async_computation.6 | async-start | bytes 5013504
  13.5 26.2 %collective-permute-start = (bf16[512,1024]{1,0:T(8,128)(2,1)S(1)}, bf16[512,1024]{1,0:T(8,128)(2,1)S(1)}, u32[]{:S(2)}, u32[]{:S(2)}) collective-permute-start(bf16[512,1024]{1,0:T(8,128)(2,1)S(1)} %copy-done.1), channel_id=1, source_target_pairs={{0,1},{1,0},{2,3},{3,2},{4,5},{5,4},{6,7},{7,6},{8,9},{9,8},{10,11... | collective-permute-start | bytes 3145736 | tf_op jit(solution)/shard_map/ppermute | solution.py:496
  72.5 2.9 copy-start
  73.6 6.1 %copy-start.8 = (bf16[512,1024]{1,0:T(8,128)(2,1)}, bf16[512,1024]{1,0:T(8,128)(2,1)S(1)}, u32[]{:S(2)}) copy-start(bf16[512,1024]{1,0:T(8,128)(2,1)S(1)} %get-tuple-element.104) | copy-start | bytes 3145732
  73.7 22.1 %copy-start.6 = (bf16[512,1024]{1,0:T(8,128)(2,1)}, bf16[512,1024]{1,0:T(8,128)(2,1)S(1)}, u32[]{:S(2)}) copy-start(bf16[512,1024]{1,0:T(8,128)(2,1)S(1)} %get-tuple-element.103) | copy-start | bytes 3145732
  82.0 13.8 %copy-start.9 = (bf16[512,1024]{1,0:T(8,128)(2,1)S(1)}, bf16[512,1024]{1,0:T(8,128)(2,1)}, u32[]{:S(2)}) copy-start(bf16[512,1024]{1,0:T(8,128)(2,1)} %copy-done.8) | copy-start | bytes 3145732
  152.9 26.2 %collective-permute-start.1 = (bf16[512,1024]{1,0:T(8,128)(2,1)S(1)}, bf16[512,1024]{1,0:T(8,128)(2,1)}, u32[]{:S(2)}, u32[]{:S(2)}) collective-permute-start(bf16[512,1024]{1,0:T(8,128)(2,1)S(1)} %convolution_convert_fusion.11), channel_id=1, source_target_pairs={{0,1},{1,0},{2,3},{3,2},{4,5},{5,4},{6,7},{7,6},{8,9},{9,8},{10,11... | collective-permute-start | bytes 3145736 | tf_op jit(solution)/shard_map/ppermute | solution.py:496
  154.4 47.1 %collective-permute-start.4 = (bf16[512,1024]{1,0:T(8,128)(2,1)}, bf16[512,1024]{1,0:T(8,128)(2,1)}, u32[]{:S(2)}, u32[]{:S(2)}) collective-permute-start(bf16[512,1024]{1,0:T(8,128)(2,1)} %param.31), channel_id=1, source_target_pairs={{0,1},{1,0},{2,3},{3,2},{4,5},{5,4},{6,7},{7,6},{8,9},{9,8},{10,11... | collective-permute-start | bytes 3145736 | tf_op jit(solution)/shard_map/ppermute | solution.py:496
  181.8 19.8 %copy-start.31 = (bf16[1024,4736]{1,0:T(8,128)(2,1)S(1)}, bf16[1024,4736]{1,0:T(8,128)(2,1)}, u32[]{:S(2)}) copy-start(bf16[1024,4736]{1,0:T(8,128)(2,1)} %all-gather.5.cloned.1.call-done) | copy-start | bytes 29097988
  182.0 52.5 %copy-start.18 = (bf16[512,1024]{1,0:T(8,128)(2,1)}, bf16[512,1024]{1,0:T(8,128)(2,1)S(1)}, u32[]{:S(2)}) copy-start(bf16[512,1024]{1,0:T(8,128)(2,1)S(1)} %multiply_convert_fusion.6) | copy-start | bytes 3145732
  182.0 41.2 %collective-permute-start.2 = (bf16[512,1024]{1,0:T(8,128)(2,1)S(1)}, bf16[512,1024]{1,0:T(8,128)(2,1)S(1)}, u32[]{:S(2)}, u32[]{:S(2)}) collective-permute-start(bf16[512,1024]{1,0:T(8,128)(2,1)S(1)} %multiply_convert_fusion.6), channel_id=1, source_target_pairs={{0,1},{1,0},{2,3},{3,2},{4,5},{5,4},{6,7},{7,6},{8,9},{9,8},{10,11... | collective-permute-start | bytes 3145736 | tf_op jit(solution)/shard_map/ppermute | solution.py:496
  233.0 24.5 %collective-permute-start.5 = (bf16[512,1024]{1,0:T(8,128)(2,1)S(1)}, bf16[512,1024]{1,0:T(8,128)(2,1)S(1)}, u32[]{:S(2)}, u32[]{:S(2)}) collective-permute-start(bf16[512,1024]{1,0:T(8,128)(2,1)S(1)} %add_convert_fusion.1), channel_id=1, source_target_pairs={{0,1},{1,0},{2,3},{3,2},{4,5},{5,4},{6,7},{7,6},{8,9},{9,8},{10,11... | collective-permute-start | bytes 3145736 | tf_op jit(solution)/shard_map/ppermute | solution.py:496
  238.5 19.0 %copy-start.35 = (bf16[512,1408]{1,0:T(8,128)(2,1)}, bf16[512,1408]{1,0:T(8,128)(2,1)S(1)}, u32[]{:S(2)}) copy-start(bf16[512,1408]{1,0:T(8,128)(2,1)S(1)} %get-tuple-element.95) | copy-start | bytes 4325380
  259.7 2.5 copy-start.2
  262.3 24.0 %copy-start.4 = (f32[1,1024,512]{2,1,0:T(8,128)S(1)}, f32[1,1024,512]{2,1,0:T(8,128)}, u32[]{:S(2)}) copy-start(f32[1,1024,512]{2,1,0:T(8,128)} %get-tuple-element.25.recalled_ref) | copy-start | bytes 6291460
  262.3 24.0 %copy-start.5 = (f32[1024,512]{1,0:T(8,128)S(1)}, f32[1024,512]{1,0:T(8,128)}, u32[]{:S(2)}) copy-start(f32[1024,512]{1,0:T(8,128)} %fusion.78) | copy-start | bytes 6291460
  262.3 23.7 %collective-permute-start.6 = (bf16[512,1024]{1,0:T(8,128)(2,1)S(1)}, bf16[512,1024]{1,0:T(8,128)(2,1)S(1)}, u32[]{:S(2)}, u32[]{:S(2)}) collective-permute-start(bf16[512,1024]{1,0:T(8,128)(2,1)S(1)} %fusion.130), channel_id=1, source_target_pairs={{0,1},{1,0},{2,3},{3,2},{4,5},{5,4},{6,7},{7,6},{8,9},{9,8},{10,11... | collective-permute-start | bytes 3145736 | tf_op jit(solution)/shard_map/ppermute | solution.py:496
  286.2 3.8 copy-start.14
  286.2 3.8 copy-start.16
  331.9 4.2 copy-start.27
  336.1 2.9 copy-start.29
  339.3 4.3 copy-start.7
  339.3 4.3 copy-start.10
  339.3 4.3 copy-start.25
  343.5 2.4 copy-start.11
  345.9 2.3 copy-start.20
  357.0 191.6 %reduce-scatter.5.cloned.1.call-start = ((), (), s32[]{:S(2)}) async-start(), calls=%async_computation.5 | async-start | bytes 10305536 | tf_op jit(solution)/shard_map/reduce_scatter | solution.py:551
  357.1 7.7 %copy-start.19 = (bf16[512,1024]{1,0:T(8,128)(2,1)S(1)}, bf16[512,1024]{1,0:T(8,128)(2,1)}, u32[]{:S(2)}) copy-start(bf16[512,1024]{1,0:T(8,128)(2,1)} %copy-done.18) | copy-start | bytes 3145732
  357.1 7.7 %copy-start.34 = (bf16[512,1024]{1,0:T(8,128)(2,1)S(1)}, bf16[512,1024]{1,0:T(8,128)(2,1)}, u32[]{:S(2)}) copy-start(bf16[512,1024]{1,0:T(8,128)(2,1)} %copy-done.33) | copy-start | bytes 3145732
  357.1 7.7 %copy-start.36 = (bf16[512,1408]{1,0:T(8,128)(2,1)S(1)}, bf16[512,1408]{1,0:T(8,128)(2,1)}, u32[]{:S(2)}) copy-start(bf16[512,1408]{1,0:T(8,128)(2,1)} %copy-done.35) | copy-start | bytes 4325380
  357.1 7.7 %copy-start.43 = (bf16[512,1408]{1,0:T(8,128)(2,1)S(1)}, bf16[512,1408]{1,0:T(8,128)(2,1)}, u32[]{:S(2)}) copy-start(bf16[512,1408]{1,0:T(8,128)(2,1)} %copy-done.42) | copy-start | bytes 4325380
  364.8 5.1 copy-start.39
  364.8 5.1 copy-start.40
  369.9 6.8 %copy-start.15 = (bf16[512,1024]{1,0:T(8,128)(2,1)S(1)}, bf16[512,1024]{1,0:T(8,128)(2,1)}, u32[]{:S(2)}) copy-start(bf16[512,1024]{1,0:T(8,128)(2,1)} %copy-done.14) | copy-start | bytes 3145732
  369.9 6.8 %copy-start.17 = (bf16[512,1024]{1,0:T(8,128)(2,1)S(1)}, bf16[512,1024]{1,0:T(8,128)(2,1)}, u32[]{:S(2)}) copy-start(bf16[512,1024]{1,0:T(8,128)(2,1)} %copy-done.16) | copy-start | bytes 3145732
  369.9 6.8 %copy-start.32 = (bf16[1,1024,512]{2,1,0:T(8,128)(2,1)S(1)}, bf16[1,1024,512]{2,1,0:T(8,128)(2,1)}, u32[]{:S(2)}) copy-start(bf16[1,1024,512]{2,1,0:T(8,128)(2,1)} %get-tuple-element.26) | copy-start | bytes 3145732
  390.5 5.7 %copy-start.26 = (bf16[1,1024,512]{2,1,0:T(8,128)(2,1)S(1)}, bf16[1,1024,512]{2,1,0:T(8,128)(2,1)}, u32[]{:S(2)}) copy-start(bf16[1,1024,512]{2,1,0:T(8,128)(2,1)} %get-tuple-element.34) | copy-start | bytes 3145732
  394.7 3.5 copy-start.23
  394.7 26.1 %collective-permute-start.3 = (bf16[512,1024]{1,0:T(8,128)(2,1)S(1)}, bf16[512,1024]{1,0:T(8,128)(2,1)S(1)}, u32[]{:S(2)}, u32[]{:S(2)}) collective-permute-start(bf16[512,1024]{1,0:T(8,128)(2,1)S(1)} %fusion.49), channel_id=1, source_target_pairs={{0,1},{1,0},{2,3},{3,2},{4,5},{5,4},{6,7},{7,6},{8,9},{9,8},{10,11... | collective-permute-start | bytes 3145736 | tf_op jit(solution)/shard_map/ppermute | solution.py:496
  402.3 18.5 %copy-start.41 = (bf16[512,1408]{1,0:T(8,128)(2,1)S(1)}, bf16[512,1408]{1,0:T(8,128)(2,1)}, u32[]{:S(2)}) copy-start(bf16[512,1408]{1,0:T(8,128)(2,1)} %get-tuple-element.96) | copy-start | bytes 4325380
  405.5 34.6 %collective-permute-start.7 = (bf16[512,1024]{1,0:T(8,128)(2,1)}, bf16[512,1024]{1,0:T(8,128)(2,1)}, u32[]{:S(2)}, u32[]{:S(2)}) collective-permute-start(bf16[512,1024]{1,0:T(8,128)(2,1)} %add_convert_fusion), channel_id=1, source_target_pairs={{0,1},{1,0},{2,3},{3,2},{4,5},{5,4},{6,7},{7,6},{8,9},{9,8},{10,11... | collective-permute-start | bytes 3145736 | tf_op jit(solution)/shard_map/ppermute | solution.py:496
  429.9 10.2 %copy-start.13 = (bf16[1024,512]{1,0:T(8,128)(2,1)S(1)}, bf16[1024,512]{1,0:T(8,128)(2,1)}, u32[]{:S(2)}) copy-start(bf16[1024,512]{1,0:T(8,128)(2,1)} %get-tuple-element.101) | copy-start | bytes 3145732
  445.2 9.8 %all-to-all-start = ((f32[16,1,128]{2,1,0:T(1,128)}), f32[16,1,128]{2,1,0:T(1,128)S(1)}, u32[]{:S(2)}, u32[]{:S(2)}) async-start(f32[16,1,128]{2,1,0:T(1,128)} %reshape.201), calls=%async_computation | async-start | bytes 16384 | tf_op jit(solution)/shard_map/all_to_all | solution.py:686
  (9 other events, 17.7 us)
Sparse Core Ops, SparseCore 0:
  11.5 55.8 all-gather.2
  69.7 81.0 all-gather.4
  357.1 73.9 reduce-scatter.6
  435.1 113.4 reduce-scatter.4
